TPU v7x, 256 devices: a whole 4x4x8 slice. The times are simulated.
256 devices in a mesh: tensor: 8 (over z), expert: 32 (over x, y, core).
Axes of the slice: x: 4, y: 4, z: 8, core: 2. Of those that a mesh axis runs over, the one named last changes fastest.
Arguments:
- queries: bfloat16 [768, 64, 576], P('expert', 'tensor'), may hold values from -200 to 200
- latent_cache_rows: bfloat16 [768, 24, 576], P('expert'), may hold values from -5 to 5
- lengths: int32 [768], P('expert'), may hold values from 6 to 24, as said below
- value_up_weight: bfloat16 [64, 512, 128], P('tensor'), may hold values from -0.25 to 0.25
- w_output: bfloat16 [8192, 7168], P('tensor', 'expert'), may hold values from -0.0625 to 0.0625
- residual: bfloat16 [768, 7168], P(None, 'expert'), may hold values from -3 to 3
- norm_gain: float32 [7168], replicated, may hold values from 0.1 to 1.9
- routes: int32 [768, 8], replicated, may hold values from 0 to 31, as said below
- gate_values: float32 [768, 8], replicated, may hold values from 0.05 to 0.5
- capacity: int32 [32], replicated, may hold values from 224 to 448, as said below
- w_gate: bfloat16 [32, 7168, 2048], P('expert', None, 'tensor'), may hold values from -0.0625 to 0.0625
- w_up: bfloat16 [32, 7168, 2048], P('expert', None, 'tensor'), may hold values from -0.0625 to 0.0625
- w_down: bfloat16 [32, 2048, 7168], P('expert', 'tensor'), may hold values from -0.125 to 0.125
Outputs:
- layer_output: bfloat16 [768, 7168], P('tensor', 'expert')
Inputs may be any that keep to these rules, and one draw needn't show every extreme that they name: Row r attends over its first lengths[r] cache slots; some row fills all 24 in every draw. `routes`: each row names 8 different experts. Some expert has capacity 448 in every draw.
All inputs are finite; a program needn't handle non-finite values.
Results may differ from a plain program's by a relative error of at most 0.0073.
Values may be sent and summed in bfloat16 or wider, within the bound.
No kernel may reach another device: no remote copies, remote signals or barrier semaphores. Data moves between devices by JAX's collectives and lax.ppermute only.
A program may use at most 128 MiB of HBM per device.

v0:
```python
import functools

import jax
import jax.numpy as jnp
from jax import lax
from jax.experimental import pallas as pl
from jax.experimental.pallas import tpu as pltpu
from jax.sharding import PartitionSpec as P

ROTARY_CHANNELS = 64
NOPE = 128
SIDE = 4
CORES = 2

epsilon = 1e-06


def place(x, y, core):
    return (x * SIDE + y) * CORES + core


def ring_groups():
    along_y = [[place(x, y, 0) for y in range(SIDE)] for x in range(SIDE)]
    along_x = [[place(x, y, 0) for x in range(SIDE)] for y in range(SIDE)]
    along_y1 = [[place(x, y, 1) for y in range(SIDE)] for x in range(SIDE)]
    along_x1 = [[place(x, y, 1) for x in range(SIDE)] for y in range(SIDE)]
    inner = along_y + along_x1
    outer = along_x + along_y1
    pairs = [[place(x, y, 0), place(x, y, 1)] for x in range(SIDE) for y in range(SIDE)]
    return inner, outer, pairs


INNER, OUTER, PAIRS = ring_groups()


def exchange(blocks, groups):
    return lax.all_to_all(blocks, "expert", 0, 0, axis_index_groups=groups, tiled=True)


def spread(block, groups, count):
    return exchange(jnp.broadcast_to(block[None], (count,) + block.shape), groups)


def gather_plane(block):
    block = spread(block, INNER, SIDE)
    block = spread(block, OUTER, SIDE)
    return spread(block, PAIRS, CORES)


def shift(block, groups, step):
    pairs = []
    for ring in groups:
        size = len(ring)
        pairs += [(ring[i], ring[(i + step) % size]) for i in range(size)]
    return lax.ppermute(block, "expert", pairs)


def add_blocks(blocks):
    return jnp.sum(blocks.astype(jnp.float32), axis=0)


def row_order(table):
    return jnp.stack([table[0], jnp.swapaxes(table[1], 0, 1)], axis=2)


def plane_tables(expert):
    x, y, core = expert // (SIDE * CORES), (expert // CORES) % SIDE, expert % CORES
    a = jnp.where(core == 0, x, y)
    b = jnp.where(core == 0, y, x)
    step = jnp.arange(SIDE, dtype=jnp.int32)

    def index(c, outer, inner):
        outer = outer % SIDE
        inner = inner % SIDE
        even = (outer * SIDE + inner) * CORES
        odd = (inner * SIDE + outer) * CORES + 1
        return jnp.where(c == 0, even, odd).astype(jnp.int32)

    k, j = step[:, None], step[None, :]
    back = SIDE - k, SIDE - j
    own_in = index(core, a + back[0], b + back[1])
    mate_in = index(1 - core, b + back[0], a + back[1])
    own_out = index(core, a + k, b + j)
    mate_out = index(1 - core, b + k, a + j)
    return own_in, mate_in, own_out, mate_out


def in_body(fresh, table, x_ref, *refs):
    gates, ups, gains = refs[:SIDE], refs[SIDE : 2 * SIDE], refs[2 * SIDE : 3 * SIDE]
    refs = refs[3 * SIDE :]
    acc_ref, sq_ref = refs[-2:]
    half = acc_ref.shape[0] // 2
    for j in range(SIDE):
        wide = x_ref[j].astype(jnp.float32)
        folded = jnp.sum((wide * wide).reshape(-1, 8, wide.shape[1]), axis=0)
        block = (wide * gains[j][0]).astype(jnp.bfloat16)
        gate = jnp.dot(gates[j][0], block, preferred_element_type=jnp.float32)
        up = jnp.dot(ups[j][0], block, preferred_element_type=jnp.float32)
        if j == 0:
            gate_sum, up_sum, square_sum = gate, up, folded
        else:
            gate_sum, up_sum, square_sum = gate_sum + gate, up_sum + up, square_sum + folded
    if not fresh:
        gate_sum += refs[0][:half]
        up_sum += refs[0][half:]
        square_sum += refs[1][...]
    acc_ref[:half] = gate_sum
    acc_ref[half:] = up_sum
    sq_ref[...] = square_sum


ROW_TILE = 256


def project_in(k, table, blocks, gate, up, gain, sums):
    count, depth, rows = blocks.shape
    units = gate.shape[1]
    keep = pl.BlockSpec((2 * units, ROW_TILE), lambda i, t: (0, i))
    keep_sq = pl.BlockSpec((8, ROW_TILE), lambda i, t: (0, i))

    def picked(shape):
        return [
            pl.BlockSpec((1,) + shape, lambda i, t, j=j: (t[k, j], 0, 0)) for j in range(count)
        ]

    in_specs = [pl.BlockSpec((count, depth, ROW_TILE), lambda i, t: (0, 0, i))]
    in_specs += picked((units, depth)) + picked((units, depth)) + picked((depth, 1))
    args = [table, blocks] + [gate] * count + [up] * count + [gain] * count
    if sums is not None:
        in_specs += [keep, keep_sq]
        args += list(sums)
    return pl.pallas_call(
        functools.partial(in_body, sums is None),
        out_shape=(
            jax.ShapeDtypeStruct((2 * units, rows), jnp.float32),
            jax.ShapeDtypeStruct((8, rows), jnp.float32),
        ),
        grid_spec=pltpu.PrefetchScalarGridSpec(
            num_scalar_prefetch=1,
            grid=(rows // ROW_TILE,),
            in_specs=in_specs,
            out_specs=(keep, keep_sq),
        ),
        compiler_params=pltpu.CompilerParams(vmem_limit_bytes=24 * 2**20),
        cost_estimate=pl.CostEstimate(
            flops=4 * count * depth * rows * units,
            bytes_accessed=2 * count * depth * (rows + 2 * units),
            transcendentals=0,
        ),
    )(*args)


def out_body(table, act_ref, scale_ref, w_ref, out_ref):
    made = jnp.dot(w_ref[0], act_ref[...], preferred_element_type=jnp.float32)
    out_ref[0] = (made * scale_ref[...]).astype(out_ref.dtype)


def out_add_body(table, act_ref, scale_ref, w_ref, mate_ref, out_ref):
    made = jnp.dot(w_ref[0], act_ref[...], preferred_element_type=jnp.float32)
    made = made * scale_ref[...] + mate_ref[0].astype(jnp.float32)
    out_ref[0] = made.astype(out_ref.dtype)


def project_out(k, table, act, scale, weights, mate=None):
    units, rows = act.shape
    depth = weights.shape[1]
    block = pl.BlockSpec((1, depth, rows), lambda i, t: (i, 0, 0))
    in_specs = [
        pl.BlockSpec((units, rows), lambda i, t: (0, 0)),
        pl.BlockSpec((1, rows), lambda i, t: (0, 0)),
        pl.BlockSpec((1, depth, units), lambda i, t: (t[k, i], 0, 0)),
    ]
    args = [table, act, scale, weights]
    if mate is not None:
        in_specs.append(block)
        args.append(mate)
    return pl.pallas_call(
        out_body if mate is None else out_add_body,
        out_shape=jax.ShapeDtypeStruct((SIDE, depth, rows), jnp.bfloat16),
        grid_spec=pltpu.PrefetchScalarGridSpec(
            num_scalar_prefetch=1, grid=(SIDE,), in_specs=in_specs, out_specs=block
        ),
        compiler_params=pltpu.CompilerParams(vmem_limit_bytes=16 * 2**20),
        cost_estimate=pl.CostEstimate(
            flops=2 * SIDE * depth * rows * units,
            bytes_accessed=2 * SIDE * depth * (rows + units),
            transcendentals=0,
        ),
    )(*args)


ORDER = (2, 1, 3)


def shards(
    queries,
    latent_cache_rows,
    lengths,
    value_up_weight,
    w_output,
    residual,
    norm_gain,
    routes,
    gate_values,
    capacity,
    w_gate,
    w_up,
    w_down,
):
    latent_width = value_up_weight.shape[1]
    softmax_scale = (NOPE + ROTARY_CHANNELS) ** (-0.5)
    scores = (
        jnp.einsum("rhc,rpc->rhp", queries, latent_cache_rows, preferred_element_type=jnp.float32)
        * softmax_scale
    )
    slot_total = latent_cache_rows.shape[1]
    live_slot = lax.broadcasted_iota(jnp.int32, (1, 1, slot_total), 2) < lengths[:, None, None]
    scores = jnp.where(live_slot, scores, -jnp.inf)
    row_peak = jnp.max(scores, axis=-1, keepdims=True)
    weight_exp = jnp.exp(scores - row_peak)
    attention_probs = (weight_exp / jnp.sum(weight_exp, axis=-1, keepdims=True)).astype(
        jnp.bfloat16
    )
    latent_rows = jnp.einsum(
        "onq,oqv->onv",
        attention_probs,
        latent_cache_rows[:, :, :latent_width],
        preferred_element_type=jnp.float32,
    ).astype(jnp.bfloat16)
    head_out = jnp.einsum(
        "rhc,hcv->rhv", latent_rows, value_up_weight, preferred_element_type=jnp.float32
    ).astype(jnp.bfloat16)
    head_rows = head_out.reshape(head_out.shape[0], -1)

    expert = lax.axis_index("expert")
    layer = lax.axis_index("tensor")
    layers = lax.axis_size("tensor")
    row_total, column_width = residual.shape
    own_rows = row_total // layers
    model_width = norm_gain.shape[0]
    hidden = w_gate.shape[2]

    named = routes == expert
    member = jnp.any(named, axis=1)
    gate_of = jnp.sum(jnp.where(named, gate_values, 0.0), axis=1)
    earlier = jnp.arange(row_total)[:, None] > jnp.arange(row_total)[None, :]
    position = jnp.dot(
        earlier.astype(jnp.bfloat16),
        member.astype(jnp.bfloat16),
        preferred_element_type=jnp.float32,
    )
    limit = capacity[expert].astype(jnp.float32)
    row_weight = jnp.where(position < limit, gate_of, 0.0)

    gain = norm_gain.reshape(-1, column_width, 1)
    gate = jnp.swapaxes(w_gate[0].reshape(-1, column_width, hidden), 1, 2)
    up = jnp.swapaxes(w_up[0].reshape(-1, column_width, hidden), 1, 2)
    down = w_down[0].T.reshape(-1, column_width, hidden)
    own_in, mate_in, own_out, mate_out = plane_tables(expert)

    heads = gather_plane(head_rows)
    partial_out = jnp.dot(
        heads.reshape(row_total, -1), w_output, preferred_element_type=jnp.float32
    )
    partial_out = partial_out.reshape(CORES, SIDE, SIDE, -1, column_width)
    partial_out = row_order(partial_out).reshape(layers, own_rows, column_width)
    parts = lax.all_to_all(partial_out.astype(jnp.bfloat16), "tensor", 0, 0, tiled=True)
    parts, gate, up = lax.optimization_barrier((parts, gate, up))
    attention = add_blocks(parts)
    own_residual = lax.dynamic_slice_in_dim(residual, layer * own_rows, own_rows, 0)
    stream = (own_residual.astype(jnp.float32) + attention).astype(jnp.bfloat16)
    columns = lax.all_to_all(
        jnp.broadcast_to(stream[None], (layers,) + stream.shape), "tensor", 0, 0, tiled=True
    )
    held = columns, down, gain, row_weight, own_in, mate_in, own_out, mate_out
    held = lax.optimization_barrier(held)
    columns, down, gain, row_weight, own_in, mate_in, own_out, mate_out = held
    columns = columns.reshape(row_total, column_width).T

    ring = [columns] + [shift(columns, INNER, k) for k in range(1, SIDE)]
    ring = jnp.stack(ring)
    arrived = {0: ring}
    for k in ORDER:
        arrived[k] = shift(ring, OUTER, k)

    def swap_in(k):
        return shift(arrived[k], PAIRS, 1)

    def add_in(table, k, block, sums):
        return project_in(k, table, block, gate, up, gain, sums)

    mates = {0: swap_in(0)}
    sums = add_in(own_in, 0, ring, None)
    sums = add_in(mate_in, 0, mates[0], sums)
    arrived[2], sums = lax.optimization_barrier((arrived[2], sums))
    mates[2] = swap_in(2)
    sums = add_in(own_in, 2, arrived[2], sums)
    sums = add_in(mate_in, 2, mates[2], sums)
    arrived[1], arrived[3], sums = lax.optimization_barrier((arrived[1], arrived[3], sums))
    mates.update({k: swap_in(k) for k in (1, 3)})
    for k in (1, 3):
        sums = add_in(own_in, k, arrived[k], sums)
    for k in (1, 3):
        sums = add_in(mate_in, k, mates[k], sums)
    total, squares = sums
    mean_square = jnp.sum(squares, axis=0, keepdims=True) / model_width
    pre = total * lax.rsqrt(mean_square + epsilon)
    activated = (jax.nn.silu(pre[:hidden]) * pre[hidden:]).astype(jnp.bfloat16)

    scale = row_weight[None, :]

    def for_mate(k):
        made = project_out(k, mate_out, activated, scale, down)
        return shift(made, PAIRS, 1)

    sums, mates = [], {2: for_mate(2)}
    for k, following in ((2, 1), (1, 3), (3, 0), (0, None)):
        if following is not None:
            mates[following] = for_mate(following)
        group = project_out(k, own_out, activated, scale, down, mates[k])
        if following is None:
            sums.append(group)
        else:
            group, activated = lax.optimization_barrier((group, activated))
            sums.append(shift(group, OUTER, k))
    parts = add_blocks(jnp.stack(sums)).astype(jnp.bfloat16)
    parts = add_blocks(
        jnp.stack([parts[0]] + [shift(parts[k], INNER, k) for k in range(1, SIDE)])
    ).astype(jnp.bfloat16)
    parts = parts.T.reshape(layers, own_rows, column_width)
    combined = add_blocks(lax.all_to_all(parts, "tensor", 0, 0, tiled=True))
    return (stream.astype(jnp.float32) + combined).astype(jnp.bfloat16)


def solution(mesh):
    in_specs = (
        P("expert", "tensor", None),
        P("expert", None, None),
        P("expert"),
        P("tensor", None, None),
        P("tensor", "expert"),
        P(None, "expert"),
        P(),
        P(),
        P(),
        P(),
        P("expert", None, "tensor"),
        P("expert", None, "tensor"),
        P("expert", "tensor", None),
    )
    out_specs = P("tensor", "expert")
    return jax.shard_map(
        shards, mesh=mesh, in_specs=in_specs, out_specs=out_specs, check_vma=False
    )
```

profile of v0, /device:TPU:2, one launch (start us, length us, event | category | flops | bytes accessed | tf_op | source)
XLA Modules:
  0.0 223.5 jit_solution(17128194787612992055)
XLA Ops:
  4.5 10.6 %all_to_all.30 = bf16[4,24,1024]{2,1,0:T(8,128)(2,1)S(1)} all-to-all(bf16[4,24,1024]{2,1,0:T(8,128)(2,1)S(1)} %broadcast_in_dim.35), channel_id=1, replica_groups={{0,2,4,6},{8,10,12,14},{16,18,20,22},{24,26,28,30},{1,9,17,25},{3,11,19..., dimensions={0} | all-to-all | bytes 393216 | tf_op jit(solution)/shard_map/all_to_all | solution.py:37
  16.1 4.8 %all-to-all-start.1 = ((bf16[4,4,24,1024]{3,2,1,0:T(8,128)(2,1)}), bf16[4,4,24,1024]{3,2,1,0:T(8,128)(2,1)S(1)}, u32[]{:S(2)}, u32[]{:S(2)}) async-start(bf16[4,4,24,1024]{3,2,1,0:T(8,128)(2,1)} %broadcast_in_dim.60), calls=%async_computation.1 | async-start | bytes 1572864 | tf_op jit(solution)/shard_map/all_to_all | solution.py:37
  21.9 7.0 %all-to-all-done.1 = bf16[4,4,24,1024]{3,2,1,0:T(8,128)(2,1)S(1)} async-done(((bf16[4,4,24,1024]{3,2,1,0:T(8,128)(2,1)}), bf16[4,4,24,1024]{3,2,1,0:T(8,128)(2,1)S(1)}, u32[]{:S(2)}, u32[]{:S(2)}) %all-to-all-start.1) | async-done | bytes 786464 | tf_op jit(solution)/shard_map/all_to_all | solution.py:37
  29.1 5.1 %all_to_all.31 = bf16[2,4,4,24,1024]{4,3,2,1,0:T(8,128)(2,1)S(1)} all-to-all(bf16[2,4,4,24,1024]{4,3,2,1,0:T(8,128)(2,1)S(1)} %broadcast_in_dim.61), channel_id=1, replica_groups={{0,1},{2,3},{4,5},{6,7},{8,9},{10,11},{12,13},{14,15},{16,17},{18,19},{..., dimensions={0} | all-to-all | bytes 3145728 | tf_op jit(solution)/shard_map/all_to_all | solution.py:37
  36.2 8.5 %all-to-all-start.3 = ((bf16[8,96,224]{2,1,0:T(8,128)(2,1)}), bf16[8,96,224]{2,1,0:T(8,128)(2,1)S(1)}, u32[]{:S(2)}, u32[]{:S(2)}) async-start(bf16[8,96,224]{2,1,0:T(8,128)(2,1)} %bitcast.6), calls=%async_computation.3 | async-start | bytes 786432 | tf_op jit(solution)/shard_map/all_to_all | solution.py:267
  44.8 6.3 %copy.25 = bf16[32,224,256]{1,2,0:T(8,128)(2,1)} copy(bf16[32,224,256]{2,1,0:T(8,128)(2,1)} %bitcast.131) | data formatting | bytes 7340032 | tf_op jit(solution)/shard_map/reshape;squeeze | solution.py:257
  51.1 6.4 %copy.24 = bf16[32,224,256]{1,2,0:T(8,128)(2,1)} copy(bf16[32,224,256]{2,1,0:T(8,128)(2,1)} %bitcast.132) | data formatting | bytes 7340032 | tf_op jit(solution)/shard_map/reshape;squeeze | solution.py:256
  60.5 5.2 %all-to-all-start.4 = ((bf16[8,96,224]{2,1,0:T(8,128)(2,1)}), bf16[8,96,224]{2,1,0:T(8,128)(2,1)S(1)}, u32[]{:S(2)}, u32[]{:S(2)}) async-start(bf16[8,96,224]{2,1,0:T(8,128)(2,1)} %broadcast_in_dim.62), calls=%async_computation.4 | async-start | bytes 786432 | tf_op jit(solution)/shard_map/all_to_all | solution.py:272
  66.9 5.8 %copy.26 = bf16[7168,256]{1,0:T(8,128)(2,1)} copy(bf16[7168,256]{0,1:T(8,128)(2,1)} %bitcast.130) | data formatting | bytes 7340032 | tf_op jit(solution)/shard_map/transpose | solution.py:258
  73.3 6.8 %all-to-all-done.4 = bf16[8,96,224]{2,1,0:T(8,128)(2,1)S(1)} async-done(((bf16[8,96,224]{2,1,0:T(8,128)(2,1)}), bf16[8,96,224]{2,1,0:T(8,128)(2,1)S(1)}, u32[]{:S(2)}, u32[]{:S(2)}) %all-to-all-start.4) | async-done | bytes 344096 | tf_op jit(solution)/shard_map/all_to_all | solution.py:272
  84.0 8.5 %collective-permute-done = bf16[224,768]{1,0:T(8,128)(2,1)S(1)} collective-permute-done((bf16[224,768]{1,0:T(8,128)(2,1)S(1)}, bf16[224,768]{1,0:T(8,128)(2,1)S(1)}, u32[]{:S(2)}, u32[]{:S(2)}) %collective-permute-start) | collective-permute-done | bytes 344096 | tf_op jit(solution)/shard_map/ppermute | solution.py:55
  107.4 3.8 %shard_map.128 = (f32[512,768]{1,0:T(8,128)S(1)}, f32[8,768]{1,0:T(8,128)S(1)}) custom-call(s32[4,4]{1,0:T(4,128)S(1)} %get-tuple-element.47.table, bf16[4,224,768]{2,1,0:T(8,128)(2,1)} %collective-permute-done.6.x_ref, bf16[32,256,224]{2,1,0:T(8,128)(2,1)S(1)} %bitcast.94, bf16[32,256,224]{2,1,0:T(8,128)(2,1)S(1)} %bitcast.95, ...), custom_call_target="tpu_custom_call" | custom-call | flops 704643072 | bytes 2293760 | tf_op jit(solution)/shard_map/pallas_call | solution.py:132
  120.8 11.1 %collective-permute-done.3.x_ref = bf16[4,224,768]{2,1,0:T(8,128)(2,1)S(1)} collective-permute-done((bf16[4,224,768]{2,1,0:T(8,128)(2,1)S(1)}, bf16[4,224,768]{2,1,0:T(8,128)(2,1)S(1)}, u32[]{:S(2)}, u32[]{:S(2)}) %collective-permute-start.3) | collective-permute-done | bytes 1376288 | tf_op jit(solution)/shard_map/ppermute | solution.py:55
  135.0 2.6 %shard_map.132 = (f32[512,768]{1,0:T(8,128)S(1)}, f32[8,768]{1,0:T(8,128)S(1)}) custom-call(s32[4,4]{1,0:T(4,128)S(1)} %get-tuple-element.52.table, bf16[4,224,768]{2,1,0:T(8,128)(2,1)S(1)} %collective-permute-done.4.x_ref, bf16[32,256,224]{2,1,0:T(8,128)(2,1)S(1)} %bitcast.110, bf16[32,256,224]{2,1,0:T(8,128)(2,1)S(1)} %bitcast.111, ...), custom_call_target="tpu_custom_call" | custom-call | flops 704643072 | bytes 2293760 | tf_op jit(solution)/shard_map/pallas_call | solution.py:132
  137.6 2.6 %shard_map.133 = (f32[512,768]{1,0:T(8,128)S(1)}, f32[8,768]{1,0:T(8,128)S(1)}) custom-call(s32[4,4]{1,0:T(4,128)S(1)} %get-tuple-element.47.table, bf16[4,224,768]{2,1,0:T(8,128)(2,1)S(1)} %collective-permute-done.9.x_ref, bf16[32,256,224]{2,1,0:T(8,128)(2,1)S(1)} %bitcast.114, bf16[32,256,224]{2,1,0:T(8,128)(2,1)S(1)} %bitcast.115, ...), custom_call_target="tpu_custom_call" | custom-call | flops 704643072 | bytes 2293760 | tf_op jit(solution)/shard_map/pallas_call | solution.py:132
  159.0 2.7 %collective-permute-start.11 = (bf16[4,224,768]{2,1,0:T(8,128)(2,1)S(1)}, bf16[4,224,768]{2,1,0:T(8,128)(2,1)S(1)}, u32[]{:S(2)}, u32[]{:S(2)}) collective-permute-start(bf16[4,224,768]{2,1,0:T(8,128)(2,1)S(1)} %shard_map.136), channel_id=1, source_target_pairs={{0,16},{8,24},{16,0},{24,8},{2,18},{10,26},{18,2},{26,10},{4,20},{... | collective-permute-start | bytes 4128776 | tf_op jit(solution)/shard_map/ppermute | solution.py:55
  163.3 2.7 %collective-permute-start.15 = (bf16[4,224,768]{2,1,0:T(8,128)(2,1)S(1)}, bf16[4,224,768]{2,1,0:T(8,128)(2,1)S(1)}, u32[]{:S(2)}, u32[]{:S(2)}) collective-permute-start(bf16[4,224,768]{2,1,0:T(8,128)(2,1)S(1)} %shard_map.140), channel_id=1, source_target_pairs={{0,24},{8,0},{16,8},{24,16},{2,26},{10,2},{18,10},{26,18},{4,28},{... | collective-permute-start | bytes 4128776 | tf_op jit(solution)/shard_map/ppermute | solution.py:55
  167.7 8.2 %collective-permute-done.13 = bf16[4,224,768]{2,1,0:T(8,128)(2,1)S(1)} collective-permute-done((bf16[4,224,768]{2,1,0:T(8,128)(2,1)S(1)}, bf16[4,224,768]{2,1,0:T(8,128)(2,1)S(1)}, u32[]{:S(2)}, u32[]{:S(2)}) %collective-permute-start.13) | collective-permute-done | bytes 1376288 | tf_op jit(solution)/shard_map/ppermute | solution.py:55
  175.9 3.0 %collective-permute-done.11 = bf16[4,224,768]{2,1,0:T(8,128)(2,1)S(1)} collective-permute-done((bf16[4,224,768]{2,1,0:T(8,128)(2,1)S(1)}, bf16[4,224,768]{2,1,0:T(8,128)(2,1)S(1)}, u32[]{:S(2)}, u32[]{:S(2)}) %collective-permute-start.11) | collective-permute-done | bytes 1376288 | tf_op jit(solution)/shard_map/ppermute | solution.py:55
  178.9 14.6 %collective-permute-done.15 = bf16[4,224,768]{2,1,0:T(8,128)(2,1)S(1)} collective-permute-done((bf16[4,224,768]{2,1,0:T(8,128)(2,1)S(1)}, bf16[4,224,768]{2,1,0:T(8,128)(2,1)S(1)}, u32[]{:S(2)}, u32[]{:S(2)}) %collective-permute-start.15) | collective-permute-done | bytes 1376288 | tf_op jit(solution)/shard_map/ppermute | solution.py:55
  194.3 3.8 %collective-permute-start.18 = (bf16[224,768]{1,0:T(8,128)(2,1)S(1)}, bf16[224,768]{1,0:T(8,128)(2,1)S(1)}, u32[]{:S(2)}, u32[]{:S(2)}) collective-permute-start(bf16[224,768]{1,0:T(8,128)(2,1)S(1)} %get-tuple-element.89), channel_id=1, source_target_pairs={{0,4},{2,6},{4,0},{6,2},{8,12},{10,14},{12,8},{14,10},{16,20},{18,... | collective-permute-start | bytes 1032200 | tf_op jit(solution)/shard_map/ppermute | solution.py:55
  198.1 4.4 %collective-permute-done.17 = bf16[224,768]{1,0:T(8,128)(2,1)S(1)} collective-permute-done((bf16[224,768]{1,0:T(8,128)(2,1)S(1)}, bf16[224,768]{1,0:T(8,128)(2,1)S(1)}, u32[]{:S(2)}, u32[]{:S(2)}) %collective-permute-start.17) | collective-permute-done | bytes 344096 | tf_op jit(solution)/shard_map/ppermute | solution.py:55
  202.4 4.5 %collective-permute-done.18 = bf16[224,768]{1,0:T(8,128)(2,1)S(1)} collective-permute-done((bf16[224,768]{1,0:T(8,128)(2,1)S(1)}, bf16[224,768]{1,0:T(8,128)(2,1)S(1)}, u32[]{:S(2)}, u32[]{:S(2)}) %collective-permute-start.18) | collective-permute-done | bytes 344096 | tf_op jit(solution)/shard_map/ppermute | solution.py:55
  207.3 15.5 %all_to_all.32 = bf16[8,96,224]{2,1,0:T(8,128)(2,1)S(1)} all-to-all(bf16[8,96,224]{2,1,0:T(8,128)(2,1)S(1)} %bitcast.135), channel_id=1, replica_groups=mesh['tensor'=8,'expert'=32] {'tensor'}, dimensions={0} | all-to-all | bytes 688128 | tf_op jit(solution)/shard_map/all_to_all | solution.py:331
  (121 shorter events, 67.9 us)
Async XLA Ops:
  16.1 12.9 %all-to-all-start.1 = ((bf16[4,4,24,1024]{3,2,1,0:T(8,128)(2,1)}), bf16[4,4,24,1024]{3,2,1,0:T(8,128)(2,1)S(1)}, u32[]{:S(2)}, u32[]{:S(2)}) async-start(bf16[4,4,24,1024]{3,2,1,0:T(8,128)(2,1)} %broadcast_in_dim.60), calls=%async_computation.1 | async-start | bytes 1572864 | tf_op jit(solution)/shard_map/all_to_all | solution.py:37
  36.2 23.5 %all-to-all-start.3 = ((bf16[8,96,224]{2,1,0:T(8,128)(2,1)}), bf16[8,96,224]{2,1,0:T(8,128)(2,1)S(1)}, u32[]{:S(2)}, u32[]{:S(2)}) async-start(bf16[8,96,224]{2,1,0:T(8,128)(2,1)} %bitcast.6), calls=%async_computation.3 | async-start | bytes 786432 | tf_op jit(solution)/shard_map/all_to_all | solution.py:267
  60.5 19.6 %all-to-all-start.4 = ((bf16[8,96,224]{2,1,0:T(8,128)(2,1)}), bf16[8,96,224]{2,1,0:T(8,128)(2,1)S(1)}, u32[]{:S(2)}, u32[]{:S(2)}) async-start(bf16[8,96,224]{2,1,0:T(8,128)(2,1)} %broadcast_in_dim.62), calls=%async_computation.4 | async-start | bytes 786432 | tf_op jit(solution)/shard_map/all_to_all | solution.py:272
  80.3 12.2 %collective-permute-start = (bf16[224,768]{1,0:T(8,128)(2,1)S(1)}, bf16[224,768]{1,0:T(8,128)(2,1)S(1)}, u32[]{:S(2)}, u32[]{:S(2)}) collective-permute-start(bf16[224,768]{1,0:T(8,128)(2,1)S(1)} %bitcast.136), channel_id=1, source_target_pairs={{0,2},{2,4},{4,6},{6,0},{8,10},{10,12},{12,14},{14,8},{16,18},{18,... | collective-permute-start | bytes 1032200 | tf_op jit(solution)/shard_map/ppermute | solution.py:55
  80.9 11.6 %collective-permute-start.1 = (bf16[224,768]{1,0:T(8,128)(2,1)S(1)}, bf16[224,768]{1,0:T(8,128)(2,1)S(1)}, u32[]{:S(2)}, u32[]{:S(2)}) collective-permute-start(bf16[224,768]{1,0:T(8,128)(2,1)S(1)} %bitcast.137), channel_id=1, source_target_pairs={{0,4},{2,6},{4,0},{6,2},{8,12},{10,14},{12,8},{14,10},{16,20},{18,... | collective-permute-start | bytes 1032200 | tf_op jit(solution)/shard_map/ppermute | solution.py:55
  83.0 10.4 %collective-permute-start.2 = (bf16[224,768]{1,0:T(8,128)(2,1)S(1)}, bf16[224,768]{1,0:T(8,128)(2,1)S(1)}, u32[]{:S(2)}, u32[]{:S(2)}) collective-permute-start(bf16[224,768]{1,0:T(8,128)(2,1)S(1)} %bitcast.138), channel_id=1, source_target_pairs={{0,6},{2,0},{4,2},{6,4},{8,14},{10,8},{12,10},{14,12},{16,22},{18,... | collective-permute-start | bytes 1032200 | tf_op jit(solution)/shard_map/ppermute | solution.py:55
  93.6 12.9 %collective-permute-start.6 = (bf16[4,224,768]{2,1,0:T(8,128)(2,1)S(1)}, bf16[4,224,768]{2,1,0:T(8,128)(2,1)}, u32[]{:S(2)}, u32[]{:S(2)}) collective-permute-start(bf16[4,224,768]{2,1,0:T(8,128)(2,1)S(1)} %pad_maximum_fusion.x_ref), channel_id=1, source_target_pairs={{0,1},{1,0},{2,3},{3,2},{4,5},{5,4},{6,7},{7,6},{8,9},{9,8},{10,11... | collective-permute-start | bytes 4128776 | tf_op jit(solution)/shard_map/ppermute | solution.py:55
  93.7 19.9 %collective-permute-start.5 = (bf16[4,224,768]{2,1,0:T(8,128)(2,1)S(1)}, bf16[4,224,768]{2,1,0:T(8,128)(2,1)S(1)}, u32[]{:S(2)}, u32[]{:S(2)}) collective-permute-start(bf16[4,224,768]{2,1,0:T(8,128)(2,1)S(1)} %pad_maximum_fusion.x_ref), channel_id=1, source_target_pairs={{0,16},{8,24},{16,0},{24,8},{2,18},{10,26},{18,2},{26,10},{4,20},{... | collective-permute-start | bytes 4128776 | tf_op jit(solution)/shard_map/ppermute | solution.py:55
  113.6 4.6 %collective-permute-start.7 = (bf16[4,224,768]{2,1,0:T(8,128)(2,1)S(1)}, bf16[4,224,768]{2,1,0:T(8,128)(2,1)S(1)}, u32[]{:S(2)}, u32[]{:S(2)}) collective-permute-start(bf16[4,224,768]{2,1,0:T(8,128)(2,1)S(1)} %collective-permute-done.5.x_ref), channel_id=1, source_target_pairs={{0,1},{1,0},{2,3},{3,2},{4,5},{5,4},{6,7},{7,6},{8,9},{9,8},{10,11... | collective-permute-start | bytes 4128776 | tf_op jit(solution)/shard_map/ppermute | solution.py:55
  113.6 18.3 %collective-permute-start.3 = (bf16[4,224,768]{2,1,0:T(8,128)(2,1)S(1)}, bf16[4,224,768]{2,1,0:T(8,128)(2,1)S(1)}, u32[]{:S(2)}, u32[]{:S(2)}) collective-permute-start(bf16[4,224,768]{2,1,0:T(8,128)(2,1)S(1)} %pad_maximum_fusion.x_ref), channel_id=1, source_target_pairs={{0,8},{8,16},{16,24},{24,0},{2,10},{10,18},{18,26},{26,2},{4,12},{... | collective-permute-start | bytes 4128776 | tf_op jit(solution)/shard_map/ppermute | solution.py:55
  113.6 18.3 %collective-permute-start.4 = (bf16[4,224,768]{2,1,0:T(8,128)(2,1)S(1)}, bf16[4,224,768]{2,1,0:T(8,128)(2,1)S(1)}, u32[]{:S(2)}, u32[]{:S(2)}) collective-permute-start(bf16[4,224,768]{2,1,0:T(8,128)(2,1)S(1)} %pad_maximum_fusion.x_ref), channel_id=1, source_target_pairs={{0,24},{8,0},{16,8},{24,16},{2,26},{10,2},{18,10},{26,18},{4,28},{... | collective-permute-start | bytes 4128776 | tf_op jit(solution)/shard_map/ppermute | solution.py:55
  131.9 5.7 %collective-permute-start.9 = (bf16[4,224,768]{2,1,0:T(8,128)(2,1)S(1)}, bf16[4,224,768]{2,1,0:T(8,128)(2,1)S(1)}, u32[]{:S(2)}, u32[]{:S(2)}) collective-permute-start(bf16[4,224,768]{2,1,0:T(8,128)(2,1)S(1)} %collective-permute-done.3.x_ref), channel_id=1, source_target_pairs={{0,1},{1,0},{2,3},{3,2},{4,5},{5,4},{6,7},{7,6},{8,9},{9,8},{10,11... | collective-permute-start | bytes 4128776 | tf_op jit(solution)/shard_map/ppermute | solution.py:55
  132.4 7.8 %collective-permute-start.8 = (bf16[4,224,768]{2,1,0:T(8,128)(2,1)S(1)}, bf16[4,224,768]{2,1,0:T(8,128)(2,1)S(1)}, u32[]{:S(2)}, u32[]{:S(2)}) collective-permute-start(bf16[4,224,768]{2,1,0:T(8,128)(2,1)S(1)} %collective-permute-done.4.x_ref), channel_id=1, source_target_pairs={{0,1},{1,0},{2,3},{3,2},{4,5},{5,4},{6,7},{7,6},{8,9},{9,8},{10,11... | collective-permute-start | bytes 4128776 | tf_op jit(solution)/shard_map/ppermute | solution.py:55
  146.5 3.3 %collective-permute-start.10 = (bf16[4,224,768]{2,1,0:T(8,128)(2,1)S(1)}, bf16[4,224,768]{2,1,0:T(8,128)(2,1)S(1)}, u32[]{:S(2)}, u32[]{:S(2)}) collective-permute-start(bf16[4,224,768]{2,1,0:T(8,128)(2,1)S(1)} %shard_map.135), channel_id=1, source_target_pairs={{0,1},{1,0},{2,3},{3,2},{4,5},{5,4},{6,7},{7,6},{8,9},{9,8},{10,11... | collective-permute-start | bytes 4128776 | tf_op jit(solution)/shard_map/ppermute | solution.py:55
  148.7 4.9 %collective-permute-start.12 = (bf16[4,224,768]{2,1,0:T(8,128)(2,1)S(1)}, bf16[4,224,768]{2,1,0:T(8,128)(2,1)S(1)}, u32[]{:S(2)}, u32[]{:S(2)}) collective-permute-start(bf16[4,224,768]{2,1,0:T(8,128)(2,1)S(1)} %shard_map.137), channel_id=1, source_target_pairs={{0,1},{1,0},{2,3},{3,2},{4,5},{5,4},{6,7},{7,6},{8,9},{9,8},{10,11... | collective-permute-start | bytes 4128776 | tf_op jit(solution)/shard_map/ppermute | solution.py:55
  153.1 8.5 %collective-permute-start.14 = (bf16[4,224,768]{2,1,0:T(8,128)(2,1)S(1)}, bf16[4,224,768]{2,1,0:T(8,128)(2,1)S(1)}, u32[]{:S(2)}, u32[]{:S(2)}) collective-permute-start(bf16[4,224,768]{2,1,0:T(8,128)(2,1)S(1)} %shard_map.139), channel_id=1, source_target_pairs={{0,1},{1,0},{2,3},{3,2},{4,5},{5,4},{6,7},{7,6},{8,9},{9,8},{10,11... | collective-permute-start | bytes 4128776 | tf_op jit(solution)/shard_map/ppermute | solution.py:55
  156.9 9.1 %collective-permute-start.16 = (bf16[4,224,768]{2,1,0:T(8,128)(2,1)S(1)}, bf16[4,224,768]{2,1,0:T(8,128)(2,1)S(1)}, u32[]{:S(2)}, u32[]{:S(2)}) collective-permute-start(bf16[4,224,768]{2,1,0:T(8,128)(2,1)S(1)} %shard_map.141), channel_id=1, source_target_pairs={{0,1},{1,0},{2,3},{3,2},{4,5},{5,4},{6,7},{7,6},{8,9},{9,8},{10,11... | collective-permute-start | bytes 4128776 | tf_op jit(solution)/shard_map/ppermute | solution.py:55
  157.1 18.8 %collective-permute-start.13 = (bf16[4,224,768]{2,1,0:T(8,128)(2,1)S(1)}, bf16[4,224,768]{2,1,0:T(8,128)(2,1)S(1)}, u32[]{:S(2)}, u32[]{:S(2)}) collective-permute-start(bf16[4,224,768]{2,1,0:T(8,128)(2,1)S(1)} %shard_map.138), channel_id=1, source_target_pairs={{0,8},{8,16},{16,24},{24,0},{2,10},{10,18},{18,26},{26,2},{4,12},{... | collective-permute-start | bytes 4128776 | tf_op jit(solution)/shard_map/ppermute | solution.py:55
  159.0 19.9 %collective-permute-start.11 = (bf16[4,224,768]{2,1,0:T(8,128)(2,1)S(1)}, bf16[4,224,768]{2,1,0:T(8,128)(2,1)S(1)}, u32[]{:S(2)}, u32[]{:S(2)}) collective-permute-start(bf16[4,224,768]{2,1,0:T(8,128)(2,1)S(1)} %shard_map.136), channel_id=1, source_target_pairs={{0,16},{8,24},{16,0},{24,8},{2,18},{10,26},{18,2},{26,10},{4,20},{... | collective-permute-start | bytes 4128776 | tf_op jit(solution)/shard_map/ppermute | solution.py:55
  163.3 30.2 %collective-permute-start.15 = (bf16[4,224,768]{2,1,0:T(8,128)(2,1)S(1)}, bf16[4,224,768]{2,1,0:T(8,128)(2,1)S(1)}, u32[]{:S(2)}, u32[]{:S(2)}) collective-permute-start(bf16[4,224,768]{2,1,0:T(8,128)(2,1)S(1)} %shard_map.140), channel_id=1, source_target_pairs={{0,24},{8,0},{16,8},{24,16},{2,26},{10,2},{18,10},{26,18},{4,28},{... | collective-permute-start | bytes 4128776 | tf_op jit(solution)/shard_map/ppermute | solution.py:55
  193.9 8.5 %collective-permute-start.17 = (bf16[224,768]{1,0:T(8,128)(2,1)S(1)}, bf16[224,768]{1,0:T(8,128)(2,1)S(1)}, u32[]{:S(2)}, u32[]{:S(2)}) collective-permute-start(bf16[224,768]{1,0:T(8,128)(2,1)S(1)} %get-tuple-element.87), channel_id=1, source_target_pairs={{0,2},{2,4},{4,6},{6,0},{8,10},{10,12},{12,14},{14,8},{16,18},{18,... | collective-permute-start | bytes 1032200 | tf_op jit(solution)/shard_map/ppermute | solution.py:55
  194.3 12.7 %collective-permute-start.18 = (bf16[224,768]{1,0:T(8,128)(2,1)S(1)}, bf16[224,768]{1,0:T(8,128)(2,1)S(1)}, u32[]{:S(2)}, u32[]{:S(2)}) collective-permute-start(bf16[224,768]{1,0:T(8,128)(2,1)S(1)} %get-tuple-element.89), channel_id=1, source_target_pairs={{0,4},{2,6},{4,0},{6,2},{8,12},{10,14},{12,8},{14,10},{16,20},{18,... | collective-permute-start | bytes 1032200 | tf_op jit(solution)/shard_map/ppermute | solution.py:55
  198.1 9.0 %collective-permute-start.19 = (bf16[224,768]{1,0:T(8,128)(2,1)S(1)}, bf16[224,768]{1,0:T(8,128)(2,1)S(1)}, u32[]{:S(2)}, u32[]{:S(2)}) collective-permute-start(bf16[224,768]{1,0:T(8,128)(2,1)S(1)} %get-tuple-element.88), channel_id=1, source_target_pairs={{0,6},{2,0},{4,2},{6,4},{8,14},{10,8},{12,10},{14,12},{16,22},{18,... | collective-permute-start | bytes 1032200 | tf_op jit(solution)/shard_map/ppermute | solution.py:55
  207.0 16.5 %copy-start.1 = (bf16[8,512,128]{2,1,0:T(8,128)(2,1)S(1)}, bf16[8,512,128]{2,1,0:T(8,128)(2,1)}, u32[]{:S(2)}) copy-start(bf16[8,512,128]{2,1,0:T(8,128)(2,1)} %param.16) | copy-start | bytes 3145732
  (12 other events, 50.5 us)
where the time goes:
time: 226 us; the launch traced here: 223 us
  waiting for transfers between devices  74.6 us (33%)
  starting transfers between devices  39.2 us (17%)
  local copies, waits for them, and re-layouts  35.3 us (16%)
  Pallas kernels  34.7 us (15%)
  blocking collectives  31.2 us (14%)
  matrix products  4.41 us (2%)
  other arithmetic  2.96 us (1%)
    ppermute x20, waiting for transfers between devices, shift(): return lax.ppermute(block, 'expert', pairs)  58.8 us
    pallas_call x8, Pallas kernels, project_in(): pl.pallas_call(functools.partial(in_body, sums is None), out_shape=(jax.S...  21.6 us
    ppermute x20, starting transfers between devices, shift(): return lax.ppermute(block, 'expert', pairs)  20.7 us
    all_to_all x2, blocking collectives, exchange(): lax.all_to_all(blocks, 'expert', 0, 0, axis_index_groups=groups, tiled=True)  15.7 us
    all_to_all x1, blocking collectives, shards(): combined = add_blocks(lax.all_to_all(parts, 'tensor', 0, 0, tiled=True))  15.5 us
    pallas_call x8, Pallas kernels, project_out(): pl.pallas_call(out_body if mate is None else out_add_body, out_shape=jax....  13.1 us
    unnamed x27, local copies, waits for them, and re-layouts  9.07 us
    all_to_all x1, starting transfers between devices, shards(): lax.all_to_all(partial_out.astype(jnp.bfloat16), 'tensor', 0, 0, tiled=True)  8.46 us
  transfers between devices with their start and end apart: 23, of which 13 were waited for; matrix products, arithmetic and copies ran while one was open for 10% of the time, Pallas kernels for 14%

commit v1 on v0

--- a/solution.py
+++ b/solution.py
@@ -85,52 +85,60 @@
     return own_in, mate_in, own_out, mate_out
 
 
-def in_body(fresh, table, x_ref, *refs):
-    gates, ups, gains = refs[:SIDE], refs[SIDE : 2 * SIDE], refs[2 * SIDE : 3 * SIDE]
-    refs = refs[3 * SIDE :]
-    acc_ref, sq_ref = refs[-2:]
-    half = acc_ref.shape[0] // 2
-    for j in range(SIDE):
-        wide = x_ref[j].astype(jnp.float32)
-        folded = jnp.sum((wide * wide).reshape(-1, 8, wide.shape[1]), axis=0)
-        block = (wide * gains[j][0]).astype(jnp.bfloat16)
-        gate = jnp.dot(gates[j][0], block, preferred_element_type=jnp.float32)
-        up = jnp.dot(ups[j][0], block, preferred_element_type=jnp.float32)
-        if j == 0:
-            gate_sum, up_sum, square_sum = gate, up, folded
-        else:
-            gate_sum, up_sum, square_sum = gate_sum + gate, up_sum + up, square_sum + folded
-    if not fresh:
-        gate_sum += refs[0][:half]
-        up_sum += refs[0][half:]
-        square_sum += refs[1][...]
-    acc_ref[:half] = gate_sum
-    acc_ref[half:] = up_sum
+def in_body(spots, fresh, table, *refs):
+    count = len(spots)
+    arrays = 1 + max(a for a, _, _ in spots)
+    blocks, refs = refs[:arrays], refs[arrays:]
+    gates, ups, gains = refs[:count], refs[count : 2 * count], refs[2 * count : 3 * count]
+    refs = refs[3 * count :]
+    acc_ref, sq_ref, left, right = refs[-4:]
+    half, step = gates[0].shape[1:]
+    depth = blocks[0].shape[1]
+
+    @pl.when(pl.program_id(0) == 0)
+    def _():
+        for c in range(count):
+            left[:half, c * step : (c + 1) * step] = gates[c][0]
+            left[half:, c * step : (c + 1) * step] = ups[c][0]
+            blank = jnp.zeros((step - depth, right.shape[1]), right.dtype)
+            right[c * step + depth : (c + 1) * step] = blank
+
+    square_sum = jnp.zeros(sq_ref.shape, jnp.float32) if fresh else refs[1][...]
+    for c, (a, row, _) in enumerate(spots):
+        wide = blocks[a][row].astype(jnp.float32)
+        square_sum += jnp.sum((wide * wide).reshape(-1, 8, wide.shape[1]), axis=0)
+        right[c * step : c * step + depth] = (wide * gains[c][0]).astype(right.dtype)
     sq_ref[...] = square_sum
+    made = jnp.dot(left[...], right[...], preferred_element_type=jnp.float32)
+    acc_ref[...] = made if fresh else made + refs[0][...]
 
 
 ROW_TILE = 256
 
 
-def project_in(k, table, blocks, gate, up, gain, sums):
-    count, depth, rows = blocks.shape
-    units = gate.shape[1]
+def project_in(spots, table, blocks, gate, up, gain, sums):
+    count = len(spots)
+    depth, rows = blocks[0].shape[1:]
+    units, step = gate.shape[1:]
     keep = pl.BlockSpec((2 * units, ROW_TILE), lambda i, t: (0, i))
     keep_sq = pl.BlockSpec((8, ROW_TILE), lambda i, t: (0, i))
 
     def picked(shape):
         return [
-            pl.BlockSpec((1,) + shape, lambda i, t, j=j: (t[k, j], 0, 0)) for j in range(count)
+            pl.BlockSpec((1,) + shape, lambda i, t, k=k, j=j: (t[k, j], 0, 0))
+            for _, _, (k, j) in spots
         ]
 
-    in_specs = [pl.BlockSpec((count, depth, ROW_TILE), lambda i, t: (0, 0, i))]
-    in_specs += picked((units, depth)) + picked((units, depth)) + picked((depth, 1))
-    args = [table, blocks] + [gate] * count + [up] * count + [gain] * count
+    in_specs = [
+        pl.BlockSpec((b.shape[0], depth, ROW_TILE), lambda i, t: (0, 0, i)) for b in blocks
+    ]
+    in_specs += picked((units, step)) + picked((units, step)) + picked((depth, 1))
+    args = [table] + list(blocks) + [gate] * count + [up] * count + [gain] * count
     if sums is not None:
         in_specs += [keep, keep_sq]
         args += list(sums)
     return pl.pallas_call(
-        functools.partial(in_body, sums is None),
+        functools.partial(in_body, spots, sums is None),
         out_shape=(
             jax.ShapeDtypeStruct((2 * units, rows), jnp.float32),
             jax.ShapeDtypeStruct((8, rows), jnp.float32),
@@ -140,8 +148,12 @@
             grid=(rows // ROW_TILE,),
             in_specs=in_specs,
             out_specs=(keep, keep_sq),
+            scratch_shapes=[
+                pltpu.VMEM((2 * units, count * step), jnp.bfloat16),
+                pltpu.VMEM((count * step, ROW_TILE), jnp.bfloat16),
+            ],
         ),
-        compiler_params=pltpu.CompilerParams(vmem_limit_bytes=24 * 2**20),
+        compiler_params=pltpu.CompilerParams(vmem_limit_bytes=32 * 2**20),
         cost_estimate=pl.CostEstimate(
             flops=4 * count * depth * rows * units,
             bytes_accessed=2 * count * depth * (rows + 2 * units),
@@ -155,10 +167,18 @@
     out_ref[0] = (made * scale_ref[...]).astype(out_ref.dtype)
 
 
-def out_add_body(table, act_ref, scale_ref, w_ref, mate_ref, out_ref):
+def out_add_body(table, act_ref, scale_ref, w_ref, mate_ref, far_ref, near_ref):
     made = jnp.dot(w_ref[0], act_ref[...], preferred_element_type=jnp.float32)
     made = made * scale_ref[...] + mate_ref[0].astype(jnp.float32)
-    out_ref[0] = made.astype(out_ref.dtype)
+    made = made.astype(far_ref.dtype)
+
+    @pl.when(pl.program_id(0) < SIDE - 1)
+    def _():
+        far_ref[0] = made
+
+    @pl.when(pl.program_id(0) == SIDE - 1)
+    def _():
+        near_ref[...] = made
 
 
 def project_out(k, table, act, scale, weights, mate=None):
@@ -168,17 +188,28 @@
     in_specs = [
         pl.BlockSpec((units, rows), lambda i, t: (0, 0)),
         pl.BlockSpec((1, rows), lambda i, t: (0, 0)),
-        pl.BlockSpec((1, depth, units), lambda i, t: (t[k, i], 0, 0)),
+        pl.BlockSpec((1, depth, units), lambda i, t: (t[k, (i + 1) % SIDE], 0, 0)),
     ]
     args = [table, act, scale, weights]
-    if mate is not None:
+    if mate is None:
+        out_shape = jax.ShapeDtypeStruct((SIDE, depth, rows), jnp.bfloat16)
+        out_specs = block
+    else:
         in_specs.append(block)
         args.append(mate)
+        out_shape = (
+            jax.ShapeDtypeStruct((SIDE - 1, depth, rows), jnp.bfloat16),
+            jax.ShapeDtypeStruct((depth, rows), jnp.bfloat16),
+        )
+        out_specs = (
+            pl.BlockSpec((1, depth, rows), lambda i, t: (jnp.minimum(i, SIDE - 2), 0, 0)),
+            pl.BlockSpec((depth, rows), lambda i, t: (0, 0)),
+        )
     return pl.pallas_call(
         out_body if mate is None else out_add_body,
-        out_shape=jax.ShapeDtypeStruct((SIDE, depth, rows), jnp.bfloat16),
+        out_shape=out_shape,
         grid_spec=pltpu.PrefetchScalarGridSpec(
-            num_scalar_prefetch=1, grid=(SIDE,), in_specs=in_specs, out_specs=block
+            num_scalar_prefetch=1, grid=(SIDE,), in_specs=in_specs, out_specs=out_specs
         ),
         compiler_params=pltpu.CompilerParams(vmem_limit_bytes=16 * 2**20),
         cost_estimate=pl.CostEstimate(
@@ -189,7 +220,8 @@
     )(*args)
 
 
-ORDER = (2, 1, 3)
+FAR = (2, 1, 3)
+PADDED = 256
 
 
 def shards(
@@ -253,8 +285,12 @@
     row_weight = jnp.where(position < limit, gate_of, 0.0)
 
     gain = norm_gain.reshape(-1, column_width, 1)
-    gate = jnp.swapaxes(w_gate[0].reshape(-1, column_width, hidden), 1, 2)
-    up = jnp.swapaxes(w_up[0].reshape(-1, column_width, hidden), 1, 2)
+
+    def turned(table):
+        blocks = jnp.swapaxes(table.reshape(-1, column_width, hidden), 1, 2)
+        return jnp.pad(blocks, ((0, 0), (0, 0), (0, PADDED - column_width)))
+
+    gate, up = turned(w_gate[0]), turned(w_up[0])
     down = w_down[0].T.reshape(-1, column_width, hidden)
     own_in, mate_in, own_out, mate_out = plane_tables(expert)
 
@@ -277,31 +313,47 @@
     columns, down, gain, row_weight, own_in, mate_in, own_out, mate_out = held
     columns = columns.reshape(row_total, column_width).T
 
-    ring = [columns] + [shift(columns, INNER, k) for k in range(1, SIDE)]
-    ring = jnp.stack(ring)
-    arrived = {0: ring}
-    for k in ORDER:
-        arrived[k] = shift(ring, OUTER, k)
-
-    def swap_in(k):
-        return shift(arrived[k], PAIRS, 1)
-
-    def add_in(table, k, block, sums):
-        return project_in(k, table, block, gate, up, gain, sums)
-
-    mates = {0: swap_in(0)}
-    sums = add_in(own_in, 0, ring, None)
-    sums = add_in(mate_in, 0, mates[0], sums)
-    arrived[2], sums = lax.optimization_barrier((arrived[2], sums))
-    mates[2] = swap_in(2)
-    sums = add_in(own_in, 2, arrived[2], sums)
-    sums = add_in(mate_in, 2, mates[2], sums)
-    arrived[1], arrived[3], sums = lax.optimization_barrier((arrived[1], arrived[3], sums))
-    mates.update({k: swap_in(k) for k in (1, 3)})
-    for k in (1, 3):
-        sums = add_in(own_in, k, arrived[k], sums)
-    for k in (1, 3):
-        sums = add_in(mate_in, k, mates[k], sums)
+    inner = []
+    for k in range(1, SIDE):
+        inner.append(shift(columns, INNER, k))
+    first, second = {}, {}
+    for k in FAR:
+        first[k] = shift(columns, OUTER, k)
+    inner = jnp.stack(inner)
+    for k in FAR:
+        second[k] = shift(inner, OUTER, k)
+
+    def swap(block):
+        return shift(block, PAIRS, 1)
+
+    def add_in(spots, table, blocks, sums):
+        return project_in(spots, table, blocks, gate, up, gain, sums)
+
+    here = ((0, 0, (0, 0)),) + tuple((1, j - 1, (0, j)) for j in range(1, SIDE))
+    ones = tuple((0, k - 1, (k, 0)) for k in range(1, SIDE))
+
+    def rest(*steps):
+        return tuple(
+            (a, j - 1, (k, j)) for a, k in enumerate(steps) for j in range(1, SIDE)
+        )
+
+    own = [columns[None], inner]
+    mate = [swap(columns)[None], swap(inner)]
+    sums = add_in(here, own_in, own, None)
+    sums = add_in(here, mate_in, mate, sums)
+    heads_of = jnp.stack([first[k] for k in range(1, SIDE)])
+    heads_of, sums = lax.optimization_barrier((heads_of, sums))
+    mate = swap(heads_of)
+    sums = add_in(ones, own_in, [heads_of], sums)
+    sums = add_in(ones, mate_in, [mate], sums)
+    second[2], sums = lax.optimization_barrier((second[2], sums))
+    mate = swap(second[2])
+    sums = add_in(rest(2), own_in, [second[2]], sums)
+    sums = add_in(rest(2), mate_in, [mate], sums)
+    second[1], second[3], sums = lax.optimization_barrier((second[1], second[3], sums))
+    mate = [swap(second[1]), swap(second[3])]
+    sums = add_in(rest(1, 3), own_in, [second[1], second[3]], sums)
+    sums = add_in(rest(1, 3), mate_in, mate, sums)
     total, squares = sums
     mean_square = jnp.sum(squares, axis=0, keepdims=True) / model_width
     pre = total * lax.rsqrt(mean_square + epsilon)
@@ -313,20 +365,25 @@
         made = project_out(k, mate_out, activated, scale, down)
         return shift(made, PAIRS, 1)
 
-    sums, mates = [], {2: for_mate(2)}
+    far, near, mates = {}, {}, {2: for_mate(2)}
     for k, following in ((2, 1), (1, 3), (3, 0), (0, None)):
         if following is not None:
             mates[following] = for_mate(following)
         group = project_out(k, own_out, activated, scale, down, mates[k])
-        if following is None:
-            sums.append(group)
+        if following is not None:
+            far[k], near[k], activated = lax.optimization_barrier((*group, activated))
         else:
-            group, activated = lax.optimization_barrier((group, activated))
-            sums.append(shift(group, OUTER, k))
-    parts = add_blocks(jnp.stack(sums)).astype(jnp.bfloat16)
-    parts = add_blocks(
-        jnp.stack([parts[0]] + [shift(parts[k], INNER, k) for k in range(1, SIDE)])
-    ).astype(jnp.bfloat16)
+            far[k], near[k] = group
+    for k in FAR:
+        far[k] = shift(far[k], OUTER, k)
+    for k in FAR:
+        near[k] = shift(near[k], OUTER, k)
+    parts = add_blocks(jnp.stack([far[k] for k in range(SIDE)])).astype(jnp.bfloat16)
+    around = []
+    for k in range(1, SIDE):
+        around.append(shift(parts[k - 1], INNER, k))
+    parts = add_blocks(jnp.stack([near[k] for k in range(SIDE)]))
+    parts = (parts + add_blocks(jnp.stack(around))).astype(jnp.bfloat16)
     parts = parts.T.reshape(layers, own_rows, column_width)
     combined = add_blocks(lax.all_to_all(parts, "tensor", 0, 0, tiled=True))
     return (stream.astype(jnp.float32) + combined).astype(jnp.bfloat16)

time: 226 us -> 242 us (1.071)
  starting transfers between devices: 39.2 us -> 48.9 us
  local copies, waits for them, and re-layouts: 35.3 us -> 44.4 us
  waiting for transfers between devices: 74.6 us -> 66.5 us
    pad x0 -> x2, local copies, waits for them, and re-layouts: none -> 8.33 us  [turned(): return jnp.pad(blocks, ((0, 0), (0, 0), (0, PADDED - column_width)))]
    ppermute x20 -> x28, starting transfers between devices: 20.7 us -> 28.4 us  [shift(): return lax.ppermute(block, 'expert', pairs)]
    ppermute x20 -> x28, waiting for transfers between devices: 58.8 us -> 52.8 us  [shift(): return lax.ppermute(block, 'expert', pairs)]
    unnamed x27 -> x31, local copies, waits for them, and re-layouts: 9.07 us -> 9.83 us
  transfers between devices with their start and end apart: 23 -> 31, of which waited for: 13 -> 13; matrix products, arithmetic and copies ran while one was open for 10% -> 14% of each run, Pallas kernels for 14% -> 12%
where the time goes in v1:
time: 242 us; the launch traced here: 239 us
  waiting for transfers between devices  66.5 us (27%)
  starting transfers between devices  48.9 us (20%)
  local copies, waits for them, and re-layouts  44.4 us (18%)
  Pallas kernels  36.5 us (15%)
  blocking collectives  33.5 us (14%)
  matrix products  4.41 us (2%)
  other arithmetic  3.33 us (1%)
    ppermute x28, waiting for transfers between devices, shift(): return lax.ppermute(block, 'expert', pairs)  52.8 us
    ppermute x28, starting transfers between devices, shift(): return lax.ppermute(block, 'expert', pairs)  28.4 us
    pallas_call x8, Pallas kernels, project_in(): pl.pallas_call(functools.partial(in_body, spots, sums is None), out_shape...  22.8 us
    all_to_all x1, blocking collectives, shards(): combined = add_blocks(lax.all_to_all(parts, 'tensor', 0, 0, tiled=True))  17.8 us
    all_to_all x2, blocking collectives, exchange(): lax.all_to_all(blocks, 'expert', 0, 0, axis_index_groups=groups, tiled=True)  15.7 us
    pallas_call x8, Pallas kernels, project_out(): pl.pallas_call(out_body if mate is None else out_add_body, out_shape=out_...  13.6 us
    another operation x2, local copies, waits for them, and re-layouts, turned(): blocks = jnp.swapaxes(table.reshape(-1, column_width, hidden), 1, 2)  12.8 us
    unnamed x31, local copies, waits for them, and re-layouts  9.83 us
  transfers between devices with their start and end apart: 31, of which 13 were waited for; matrix products, arithmetic and copies ran while one was open for 14% of the time, Pallas kernels for 12%

profile of v1, /device:TPU:2, one launch (start us, length us, event | category | flops | bytes accessed | tf_op | source)
XLA Modules:
  0.0 238.7 jit_solution(11291697210978725835)
XLA Ops:
  4.5 10.6 %all_to_all.30 = bf16[4,24,1024]{2,1,0:T(8,128)(2,1)S(1)} all-to-all(bf16[4,24,1024]{2,1,0:T(8,128)(2,1)S(1)} %broadcast_in_dim.65), channel_id=1, replica_groups={{0,2,4,6},{8,10,12,14},{16,18,20,22},{24,26,28,30},{1,9,17,25},{3,11,19..., dimensions={0} | all-to-all | bytes 393216 | tf_op jit(solution)/shard_map/all_to_all | solution.py:37
  16.1 4.8 %all-to-all-start.1 = ((bf16[4,4,24,1024]{3,2,1,0:T(8,128)(2,1)}), bf16[4,4,24,1024]{3,2,1,0:T(8,128)(2,1)S(1)}, u32[]{:S(2)}, u32[]{:S(2)}) async-start(bf16[4,4,24,1024]{3,2,1,0:T(8,128)(2,1)} %broadcast_in_dim.66), calls=%async_computation.1 | async-start | bytes 1572864 | tf_op jit(solution)/shard_map/all_to_all | solution.py:37
  22.0 7.0 %all-to-all-done.1 = bf16[4,4,24,1024]{3,2,1,0:T(8,128)(2,1)S(1)} async-done(((bf16[4,4,24,1024]{3,2,1,0:T(8,128)(2,1)}), bf16[4,4,24,1024]{3,2,1,0:T(8,128)(2,1)S(1)}, u32[]{:S(2)}, u32[]{:S(2)}) %all-to-all-start.1) | async-done | bytes 786464 | tf_op jit(solution)/shard_map/all_to_all | solution.py:37
  29.1 5.1 %all_to_all.31 = bf16[2,4,4,24,1024]{4,3,2,1,0:T(8,128)(2,1)S(1)} all-to-all(bf16[2,4,4,24,1024]{4,3,2,1,0:T(8,128)(2,1)S(1)} %broadcast_in_dim.67), channel_id=1, replica_groups={{0,1},{2,3},{4,5},{6,7},{8,9},{10,11},{12,13},{14,15},{16,17},{18,19},{..., dimensions={0} | all-to-all | bytes 3145728 | tf_op jit(solution)/shard_map/all_to_all | solution.py:37
  36.2 8.5 %all-to-all-start.3 = ((bf16[8,96,224]{2,1,0:T(8,128)(2,1)}), bf16[8,96,224]{2,1,0:T(8,128)(2,1)S(1)}, u32[]{:S(2)}, u32[]{:S(2)}) async-start(bf16[8,96,224]{2,1,0:T(8,128)(2,1)} %bitcast.6), calls=%async_computation.3 | async-start | bytes 786432 | tf_op jit(solution)/shard_map/all_to_all | solution.py:303
  44.8 6.4 %copy.67 = bf16[32,224,256]{1,2,0:T(8,128)(2,1)} copy(bf16[32,224,256]{2,1,0:T(8,128)(2,1)} %bitcast.80) | data formatting | bytes 7340032 | tf_op jit(solution)/shard_map/reshape;squeeze | solution.py:290
  51.1 6.4 %copy.68 = bf16[32,224,256]{1,2,0:T(8,128)(2,1)} copy(bf16[32,224,256]{2,1,0:T(8,128)(2,1)} %bitcast.81) | data formatting | bytes 7340032 | tf_op jit(solution)/shard_map/reshape;squeeze | solution.py:290
  57.5 5.3 %pad.7.refs_2_.refs_3_.refs_4_.refs_5_.refs_1_.refs_6_.refs_7_ = bf16[32,256,256]{2,1,0:T(8,128)(2,1)} pad(bf16[32,256,224]{2,1,0:T(8,128)(2,1)} %bitcast.78, bf16[]{:T(256)} %constant.116.clone.1), padding=0_0x0_0x0_32 | pad | bytes 7864322 | tf_op jit(solution)/shard_map/jit(_pad)/pad | solution.py:291
  62.8 3.0 %pad.8.refs_6_.refs_7_.refs_8_.refs_9_.refs_4_.refs_5_.refs_10_.refs_11_.refs_12_.refs_13_ = bf16[32,256,256]{2,1,0:T(8,128)(2,1)} pad(bf16[32,256,224]{2,1,0:T(8,128)(2,1)S(1)} %bitcast.77, bf16[]{:T(256)} %constant.116.clone.1), padding=0_0x0_0x0_32 | pad | bytes 7864322 | tf_op jit(solution)/shard_map/jit(_pad)/pad | solution.py:291
  66.9 7.2 %all-to-all-start.4 = ((bf16[8,96,224]{2,1,0:T(8,128)(2,1)}), bf16[8,96,224]{2,1,0:T(8,128)(2,1)S(1)}, u32[]{:S(2)}, u32[]{:S(2)}) async-start(bf16[8,96,224]{2,1,0:T(8,128)(2,1)} %broadcast_in_dim.68), calls=%async_computation.4 | async-start | bytes 786432 | tf_op jit(solution)/shard_map/all_to_all | solution.py:308
  75.4 5.9 %copy.69 = bf16[7168,256]{1,0:T(8,128)(2,1)} copy(bf16[7168,256]{0,1:T(8,128)(2,1)} %bitcast.79) | data formatting | bytes 7340032 | tf_op jit(solution)/shard_map/transpose | solution.py:294
  81.7 6.7 %all-to-all-done.4 = bf16[8,96,224]{2,1,0:T(8,128)(2,1)S(1)} async-done(((bf16[8,96,224]{2,1,0:T(8,128)(2,1)}), bf16[8,96,224]{2,1,0:T(8,128)(2,1)S(1)}, u32[]{:S(2)}, u32[]{:S(2)}) %all-to-all-start.4) | async-done | bytes 344096 | tf_op jit(solution)/shard_map/all_to_all | solution.py:308
  92.4 8.5 %collective-permute-done = bf16[224,768]{1,0:T(8,128)(2,1)S(1)} collective-permute-done((bf16[224,768]{1,0:T(8,128)(2,1)S(1)}, bf16[224,768]{1,0:T(8,128)(2,1)S(1)}, u32[]{:S(2)}, u32[]{:S(2)}) %collective-permute-start) | collective-permute-done | bytes 344096 | tf_op jit(solution)/shard_map/ppermute | solution.py:55
  102.1 3.5 %collective-permute-start.7 = (bf16[224,768]{1,0:T(8,128)(2,1)S(1)}, bf16[224,768]{1,0:T(8,128)(2,1)S(1)}, u32[]{:S(2)}, u32[]{:S(2)}) collective-permute-start(bf16[224,768]{1,0:T(8,128)(2,1)S(1)} %bitcast.71), channel_id=1, source_target_pairs={{0,16},{8,24},{16,0},{24,8},{2,18},{10,26},{18,2},{26,10},{4,20},{... | collective-permute-start | bytes 1032200 | tf_op jit(solution)/shard_map/ppermute | solution.py:55
  119.6 3.9 %shard_map.128 = (f32[512,768]{1,0:T(8,128)S(1)}, f32[8,768]{1,0:T(8,128)S(1)}) custom-call(s32[4,4]{1,0:T(4,128)S(1)} %get-tuple-element.61.table, bf16[1,224,768]{2,1,0:T(8,128)(2,1)S(1)} %bitcast.75, bf16[3,224,768]{2,1,0:T(8,128)(2,1)} %collective-permute-done.10.refs_1_, bf16[32,256,256]{2,1,0:T(8,128)(2,1)S(1)} %copy-done.3, ...), custom_call_target="tpu_custom_call" | custom-call | flops 704643072 | bytes 2293760 | tf_op jit(solution)/shard_map/pallas_call | solution.py:140
  129.8 10.3 %collective-permute-done.5.refs_0_ = bf16[3,224,768]{2,1,0:T(8,128)(2,1)S(1)} collective-permute-done((bf16[3,224,768]{2,1,0:T(8,128)(2,1)S(1)}, bf16[3,224,768]{2,1,0:T(8,128)(2,1)S(1)}, u32[]{:S(2)}, u32[]{:S(2)}) %collective-permute-start.5) | collective-permute-done | bytes 1032224 | tf_op jit(solution)/shard_map/ppermute | solution.py:55
  147.1 7.7 %collective-permute-done.3.refs_0_ = bf16[3,224,768]{2,1,0:T(8,128)(2,1)S(1)} collective-permute-done((bf16[3,224,768]{2,1,0:T(8,128)(2,1)S(1)}, bf16[3,224,768]{2,1,0:T(8,128)(2,1)S(1)}, u32[]{:S(2)}, u32[]{:S(2)}) %collective-permute-start.3) | collective-permute-done | bytes 1032224 | tf_op jit(solution)/shard_map/ppermute | solution.py:55
  156.8 3.3 %shard_map.133 = (f32[512,768]{1,0:T(8,128)S(1)}, f32[8,768]{1,0:T(8,128)S(1)}) custom-call(s32[4,4]{1,0:T(4,128)S(1)} %get-tuple-element.66.table, bf16[3,224,768]{2,1,0:T(8,128)(2,1)S(1)} %collective-permute-done.3.refs_0_, bf16[3,224,768]{2,1,0:T(8,128)(2,1)S(1)} %collective-permute-done.4.refs_1_, bf16[32,256,256]{2,1,0:T(8,128)(2,1)S(1)} %copy-done.3, ...), custom_call_target="tpu_custom_call" | custom-call | flops 1056964608 | bytes 3440640 | tf_op jit(solution)/shard_map/pallas_call | solution.py:140
  160.4 3.3 %shard_map.134 = (f32[512,768]{1,0:T(8,128)S(1)}, f32[8,768]{1,0:T(8,128)S(1)}) custom-call(s32[4,4]{1,0:T(4,128)S(1)} %get-tuple-element.61.table, bf16[3,224,768]{2,1,0:T(8,128)(2,1)S(1)} %collective-permute-done.13.refs_0_, bf16[3,224,768]{2,1,0:T(8,128)(2,1)S(1)} %collective-permute-done.14.refs_1_, bf16[32,256,256]{2,1,0:T(8,128)(2,1)S(1)} %copy-done.3, ...), custom_call_target="tpu_custom_call" | custom-call | flops 1056964608 | bytes 3440640 | tf_op jit(solution)/shard_map/pallas_call | solution.py:140
  189.3 3.5 %collective-permute-done.22 = bf16[3,224,768]{2,1,0:T(8,128)(2,1)S(1)} collective-permute-done((bf16[3,224,768]{2,1,0:T(8,128)(2,1)S(1)}, bf16[3,224,768]{2,1,0:T(8,128)(2,1)S(1)}, u32[]{:S(2)}, u32[]{:S(2)}) %collective-permute-start.22) | collective-permute-done | bytes 1032224 | tf_op jit(solution)/shard_map/ppermute | solution.py:55
  194.6 10.9 %collective-permute-done.24 = bf16[3,224,768]{2,1,0:T(8,128)(2,1)S(1)} collective-permute-done((bf16[3,224,768]{2,1,0:T(8,128)(2,1)S(1)}, bf16[3,224,768]{2,1,0:T(8,128)(2,1)S(1)}, u32[]{:S(2)}, u32[]{:S(2)}) %collective-permute-start.24) | collective-permute-done | bytes 1032224 | tf_op jit(solution)/shard_map/ppermute | solution.py:55
  207.5 2.8 %collective-permute-start.26 = (bf16[224,768]{1,0:T(8,128)(2,1)S(1)}, bf16[224,768]{1,0:T(8,128)(2,1)S(1)}, u32[]{:S(2)}, u32[]{:S(2)}) collective-permute-start(bf16[224,768]{1,0:T(8,128)(2,1)S(1)} %get-tuple-element.117), channel_id=1, source_target_pairs={{0,4},{2,6},{4,0},{6,2},{8,12},{10,14},{12,8},{14,10},{16,20},{18,... | collective-permute-start | bytes 1032200 | tf_op jit(solution)/shard_map/ppermute | solution.py:55
  211.1 8.2 %collective-permute-done.21 = bf16[224,768]{1,0:T(8,128)(2,1)S(1)} collective-permute-done((bf16[224,768]{1,0:T(8,128)(2,1)S(1)}, bf16[224,768]{1,0:T(8,128)(2,1)S(1)}, u32[]{:S(2)}, u32[]{:S(2)}) %collective-permute-start.21) | collective-permute-done | bytes 344096 | tf_op jit(solution)/shard_map/ppermute | solution.py:55
  220.3 17.8 %all_to_all.32 = bf16[8,96,224]{2,1,0:T(8,128)(2,1)S(1)} all-to-all(bf16[8,96,224]{2,1,0:T(8,128)(2,1)S(1)} %bitcast.84), channel_id=1, replica_groups=mesh['tensor'=8,'expert'=32] {'tensor'}, dimensions={0} | all-to-all | bytes 688128 | tf_op jit(solution)/shard_map/all_to_all | solution.py:388
  (146 shorter events, 77.0 us)
Async XLA Ops:
  16.1 12.9 %all-to-all-start.1 = ((bf16[4,4,24,1024]{3,2,1,0:T(8,128)(2,1)}), bf16[4,4,24,1024]{3,2,1,0:T(8,128)(2,1)S(1)}, u32[]{:S(2)}, u32[]{:S(2)}) async-start(bf16[4,4,24,1024]{3,2,1,0:T(8,128)(2,1)} %broadcast_in_dim.66), calls=%async_computation.1 | async-start | bytes 1572864 | tf_op jit(solution)/shard_map/all_to_all | solution.py:37
  36.2 29.8 %all-to-all-start.3 = ((bf16[8,96,224]{2,1,0:T(8,128)(2,1)}), bf16[8,96,224]{2,1,0:T(8,128)(2,1)S(1)}, u32[]{:S(2)}, u32[]{:S(2)}) async-start(bf16[8,96,224]{2,1,0:T(8,128)(2,1)} %bitcast.6), calls=%async_computation.3 | async-start | bytes 786432 | tf_op jit(solution)/shard_map/all_to_all | solution.py:303
  66.9 21.6 %all-to-all-start.4 = ((bf16[8,96,224]{2,1,0:T(8,128)(2,1)}), bf16[8,96,224]{2,1,0:T(8,128)(2,1)S(1)}, u32[]{:S(2)}, u32[]{:S(2)}) async-start(bf16[8,96,224]{2,1,0:T(8,128)(2,1)} %broadcast_in_dim.68), calls=%async_computation.4 | async-start | bytes 786432 | tf_op jit(solution)/shard_map/all_to_all | solution.py:308
  88.7 12.2 %collective-permute-start = (bf16[224,768]{1,0:T(8,128)(2,1)S(1)}, bf16[224,768]{1,0:T(8,128)(2,1)S(1)}, u32[]{:S(2)}, u32[]{:S(2)}) collective-permute-start(bf16[224,768]{1,0:T(8,128)(2,1)S(1)} %bitcast.67), channel_id=1, source_target_pairs={{0,2},{2,4},{4,6},{6,0},{8,10},{10,12},{12,14},{14,8},{16,18},{18,... | collective-permute-start | bytes 1032200 | tf_op jit(solution)/shard_map/ppermute | solution.py:55
  89.3 11.6 %collective-permute-start.1 = (bf16[224,768]{1,0:T(8,128)(2,1)S(1)}, bf16[224,768]{1,0:T(8,128)(2,1)S(1)}, u32[]{:S(2)}, u32[]{:S(2)}) collective-permute-start(bf16[224,768]{1,0:T(8,128)(2,1)S(1)} %bitcast.68), channel_id=1, source_target_pairs={{0,4},{2,6},{4,0},{6,2},{8,12},{10,14},{12,8},{14,10},{16,20},{18,... | collective-permute-start | bytes 1032200 | tf_op jit(solution)/shard_map/ppermute | solution.py:55
  91.4 10.4 %collective-permute-start.2 = (bf16[224,768]{1,0:T(8,128)(2,1)S(1)}, bf16[224,768]{1,0:T(8,128)(2,1)S(1)}, u32[]{:S(2)}, u32[]{:S(2)}) collective-permute-start(bf16[224,768]{1,0:T(8,128)(2,1)S(1)} %bitcast.69), channel_id=1, source_target_pairs={{0,6},{2,0},{4,2},{6,4},{8,14},{10,8},{12,10},{14,12},{16,22},{18,... | collective-permute-start | bytes 1032200 | tf_op jit(solution)/shard_map/ppermute | solution.py:55
  101.9 16.0 %collective-permute-start.10 = (bf16[3,224,768]{2,1,0:T(8,128)(2,1)S(1)}, bf16[3,224,768]{2,1,0:T(8,128)(2,1)}, u32[]{:S(2)}, u32[]{:S(2)}) collective-permute-start(bf16[3,224,768]{2,1,0:T(8,128)(2,1)S(1)} %pad_maximum_fusion.refs_1_), channel_id=1, source_target_pairs={{0,1},{1,0},{2,3},{3,2},{4,5},{5,4},{6,7},{7,6},{8,9},{9,8},{10,11... | collective-permute-start | bytes 3096584 | tf_op jit(solution)/shard_map/ppermute | solution.py:55
  102.0 15.8 %collective-permute-start.6 = (bf16[224,768]{1,0:T(8,128)(2,1)S(1)}, bf16[224,768]{1,0:T(8,128)(2,1)S(1)}, u32[]{:S(2)}, u32[]{:S(2)}) collective-permute-start(bf16[224,768]{1,0:T(8,128)(2,1)S(1)} %bitcast.70), channel_id=1, source_target_pairs={{0,8},{8,16},{16,24},{24,0},{2,10},{10,18},{18,26},{26,2},{4,12},{... | collective-permute-start | bytes 1032200 | tf_op jit(solution)/shard_map/ppermute | solution.py:55
  102.1 15.7 %collective-permute-start.7 = (bf16[224,768]{1,0:T(8,128)(2,1)S(1)}, bf16[224,768]{1,0:T(8,128)(2,1)S(1)}, u32[]{:S(2)}, u32[]{:S(2)}) collective-permute-start(bf16[224,768]{1,0:T(8,128)(2,1)S(1)} %bitcast.71), channel_id=1, source_target_pairs={{0,16},{8,24},{16,0},{24,8},{2,18},{10,26},{18,2},{26,10},{4,20},{... | collective-permute-start | bytes 1032200 | tf_op jit(solution)/shard_map/ppermute | solution.py:55
  105.6 12.2 %collective-permute-start.8 = (bf16[224,768]{1,0:T(8,128)(2,1)S(1)}, bf16[224,768]{1,0:T(8,128)(2,1)S(1)}, u32[]{:S(2)}, u32[]{:S(2)}) collective-permute-start(bf16[224,768]{1,0:T(8,128)(2,1)S(1)} %bitcast.72), channel_id=1, source_target_pairs={{0,24},{8,0},{16,8},{24,16},{2,26},{10,2},{18,10},{26,18},{4,28},{... | collective-permute-start | bytes 1032200 | tf_op jit(solution)/shard_map/ppermute | solution.py:55
  106.2 11.7 %collective-permute-start.9 = (bf16[224,768]{1,0:T(8,128)(2,1)S(1)}, bf16[224,768]{1,0:T(8,128)(2,1)S(1)}, u32[]{:S(2)}, u32[]{:S(2)}) collective-permute-start(bf16[224,768]{1,0:T(8,128)(2,1)S(1)} %bitcast.73), channel_id=1, source_target_pairs={{0,1},{1,0},{2,3},{3,2},{4,5},{5,4},{6,7},{7,6},{8,9},{9,8},{10,11... | collective-permute-start | bytes 1032200 | tf_op jit(solution)/shard_map/ppermute | solution.py:55
  124.0 16.1 %collective-permute-start.5 = (bf16[3,224,768]{2,1,0:T(8,128)(2,1)S(1)}, bf16[3,224,768]{2,1,0:T(8,128)(2,1)S(1)}, u32[]{:S(2)}, u32[]{:S(2)}) collective-permute-start(bf16[3,224,768]{2,1,0:T(8,128)(2,1)S(1)} %pad_maximum_fusion.refs_1_), channel_id=1, source_target_pairs={{0,16},{8,24},{16,0},{24,8},{2,18},{10,26},{18,2},{26,10},{4,20},{... | collective-permute-start | bytes 3096584 | tf_op jit(solution)/shard_map/ppermute | solution.py:55
  140.2 14.6 %collective-permute-start.3 = (bf16[3,224,768]{2,1,0:T(8,128)(2,1)S(1)}, bf16[3,224,768]{2,1,0:T(8,128)(2,1)S(1)}, u32[]{:S(2)}, u32[]{:S(2)}) collective-permute-start(bf16[3,224,768]{2,1,0:T(8,128)(2,1)S(1)} %pad_maximum_fusion.refs_1_), channel_id=1, source_target_pairs={{0,8},{8,16},{16,24},{24,0},{2,10},{10,18},{18,26},{26,2},{4,12},{... | collective-permute-start | bytes 3096584 | tf_op jit(solution)/shard_map/ppermute | solution.py:55
  141.6 14.6 %collective-permute-start.4 = (bf16[3,224,768]{2,1,0:T(8,128)(2,1)S(1)}, bf16[3,224,768]{2,1,0:T(8,128)(2,1)S(1)}, u32[]{:S(2)}, u32[]{:S(2)}) collective-permute-start(bf16[3,224,768]{2,1,0:T(8,128)(2,1)S(1)} %pad_maximum_fusion.refs_1_), channel_id=1, source_target_pairs={{0,24},{8,0},{16,8},{24,16},{2,26},{10,2},{18,10},{26,18},{4,28},{... | collective-permute-start | bytes 3096584 | tf_op jit(solution)/shard_map/ppermute | solution.py:55
  177.7 7.7 %collective-permute-start.18 = (bf16[4,224,768]{2,1,0:T(8,128)(2,1)S(1)}, bf16[4,224,768]{2,1,0:T(8,128)(2,1)S(1)}, u32[]{:S(2)}, u32[]{:S(2)}) collective-permute-start(bf16[4,224,768]{2,1,0:T(8,128)(2,1)S(1)} %shard_map.141), channel_id=1, source_target_pairs={{0,1},{1,0},{2,3},{3,2},{4,5},{5,4},{6,7},{7,6},{8,9},{9,8},{10,11... | collective-permute-start | bytes 4128776 | tf_op jit(solution)/shard_map/ppermute | solution.py:55
  178.1 14.6 %collective-permute-start.22 = (bf16[3,224,768]{2,1,0:T(8,128)(2,1)S(1)}, bf16[3,224,768]{2,1,0:T(8,128)(2,1)S(1)}, u32[]{:S(2)}, u32[]{:S(2)}) collective-permute-start(bf16[3,224,768]{2,1,0:T(8,128)(2,1)S(1)} %get-tuple-element.110), channel_id=1, source_target_pairs={{0,8},{8,16},{16,24},{24,0},{2,10},{10,18},{18,26},{26,2},{4,12},{... | collective-permute-start | bytes 3096584 | tf_op jit(solution)/shard_map/ppermute | solution.py:55
  178.3 16.3 %collective-permute-start.23 = (bf16[3,224,768]{2,1,0:T(8,128)(2,1)S(1)}, bf16[3,224,768]{2,1,0:T(8,128)(2,1)S(1)}, u32[]{:S(2)}, u32[]{:S(2)}) collective-permute-start(bf16[3,224,768]{2,1,0:T(8,128)(2,1)S(1)} %get-tuple-element.111), channel_id=1, source_target_pairs={{0,16},{8,24},{16,0},{24,8},{2,18},{10,26},{18,2},{26,10},{4,20},{... | collective-permute-start | bytes 3096584 | tf_op jit(solution)/shard_map/ppermute | solution.py:55
  182.6 22.9 %collective-permute-start.24 = (bf16[3,224,768]{2,1,0:T(8,128)(2,1)S(1)}, bf16[3,224,768]{2,1,0:T(8,128)(2,1)S(1)}, u32[]{:S(2)}, u32[]{:S(2)}) collective-permute-start(bf16[3,224,768]{2,1,0:T(8,128)(2,1)S(1)} %get-tuple-element.112), channel_id=1, source_target_pairs={{0,24},{8,0},{16,8},{24,16},{2,26},{10,2},{18,10},{26,18},{4,28},{... | collective-permute-start | bytes 3096584 | tf_op jit(solution)/shard_map/ppermute | solution.py:55
  185.3 24.9 %collective-permute-start.19 = (bf16[224,768]{1,0:T(8,128)(2,1)S(1)}, bf16[224,768]{1,0:T(8,128)(2,1)S(1)}, u32[]{:S(2)}, u32[]{:S(2)}) collective-permute-start(bf16[224,768]{1,0:T(8,128)(2,1)S(1)} %get-tuple-element.106), channel_id=1, source_target_pairs={{0,8},{8,16},{16,24},{24,0},{2,10},{10,18},{18,26},{26,2},{4,12},{... | collective-permute-start | bytes 1032200 | tf_op jit(solution)/shard_map/ppermute | solution.py:55
  185.3 25.8 %collective-permute-start.20 = (bf16[224,768]{1,0:T(8,128)(2,1)S(1)}, bf16[224,768]{1,0:T(8,128)(2,1)S(1)}, u32[]{:S(2)}, u32[]{:S(2)}) collective-permute-start(bf16[224,768]{1,0:T(8,128)(2,1)S(1)} %get-tuple-element.107), channel_id=1, source_target_pairs={{0,16},{8,24},{16,0},{24,8},{2,18},{10,26},{18,2},{26,10},{4,20},{... | collective-permute-start | bytes 1032200 | tf_op jit(solution)/shard_map/ppermute | solution.py:55
  192.7 26.5 %collective-permute-start.21 = (bf16[224,768]{1,0:T(8,128)(2,1)S(1)}, bf16[224,768]{1,0:T(8,128)(2,1)S(1)}, u32[]{:S(2)}, u32[]{:S(2)}) collective-permute-start(bf16[224,768]{1,0:T(8,128)(2,1)S(1)} %get-tuple-element.108), channel_id=1, source_target_pairs={{0,24},{8,0},{16,8},{24,16},{2,26},{10,2},{18,10},{26,18},{4,28},{... | collective-permute-start | bytes 1032200 | tf_op jit(solution)/shard_map/ppermute | solution.py:55
  205.8 13.7 %collective-permute-start.25 = (bf16[224,768]{1,0:T(8,128)(2,1)S(1)}, bf16[224,768]{1,0:T(8,128)(2,1)S(1)}, u32[]{:S(2)}, u32[]{:S(2)}) collective-permute-start(bf16[224,768]{1,0:T(8,128)(2,1)S(1)} %get-tuple-element.115), channel_id=1, source_target_pairs={{0,2},{2,4},{4,6},{6,0},{8,10},{10,12},{12,14},{14,8},{16,18},{18,... | collective-permute-start | bytes 1032200 | tf_op jit(solution)/shard_map/ppermute | solution.py:55
  207.5 12.4 %collective-permute-start.26 = (bf16[224,768]{1,0:T(8,128)(2,1)S(1)}, bf16[224,768]{1,0:T(8,128)(2,1)S(1)}, u32[]{:S(2)}, u32[]{:S(2)}) collective-permute-start(bf16[224,768]{1,0:T(8,128)(2,1)S(1)} %get-tuple-element.117), channel_id=1, source_target_pairs={{0,4},{2,6},{4,0},{6,2},{8,12},{10,14},{12,8},{14,10},{16,20},{18,... | collective-permute-start | bytes 1032200 | tf_op jit(solution)/shard_map/ppermute | solution.py:55
  210.3 9.6 %collective-permute-start.27 = (bf16[224,768]{1,0:T(8,128)(2,1)S(1)}, bf16[224,768]{1,0:T(8,128)(2,1)S(1)}, u32[]{:S(2)}, u32[]{:S(2)}) collective-permute-start(bf16[224,768]{1,0:T(8,128)(2,1)S(1)} %get-tuple-element.116), channel_id=1, source_target_pairs={{0,6},{2,0},{4,2},{6,4},{8,14},{10,8},{12,10},{14,12},{16,22},{18,... | collective-permute-start | bytes 1032200 | tf_op jit(solution)/shard_map/ppermute | solution.py:55
  (22 other events, 104.5 us)

commit v2 on v1

--- a/solution.py
+++ b/solution.py
@@ -89,25 +89,36 @@
     count = len(spots)
     arrays = 1 + max(a for a, _, _ in spots)
     blocks, refs = refs[:arrays], refs[arrays:]
-    gates, ups, gains = refs[:count], refs[count : 2 * count], refs[2 * count : 3 * count]
-    refs = refs[3 * count :]
-    acc_ref, sq_ref, left, right = refs[-4:]
-    half, step = gates[0].shape[1:]
-    depth = blocks[0].shape[1]
+    sources, gains = refs[:2], refs[2 : 2 + count]
+    refs = refs[2 + count :]
+    acc_ref, sq_ref, left, right, held, sems = refs[-6:]
+    half, depth = sources[0].shape[1:]
+    step = PADDED
 
     @pl.when(pl.program_id(0) == 0)
     def _():
+        copies = []
+        for c, (_, _, (m, k, j)) in enumerate(spots):
+            for side in range(2):
+                source = sources[side].at[table[m, k, j]]
+                copy = pltpu.make_async_copy(source, held.at[c, side], sems.at[c, side])
+                copy.start()
+                copies.append(copy)
+        for copy in copies:
+            copy.wait()
         for c in range(count):
-            left[:half, c * step : (c + 1) * step] = gates[c][0]
-            left[half:, c * step : (c + 1) * step] = ups[c][0]
-            blank = jnp.zeros((step - depth, right.shape[1]), right.dtype)
-            right[c * step + depth : (c + 1) * step] = blank
+            low, edge, high = c * step, c * step + depth, (c + 1) * step
+            left[:half, low:edge] = held[c, 0]
+            left[half:, low:edge] = held[c, 1]
+            left[:, edge:high] = jnp.zeros((2 * half, step - depth), left.dtype)
+            right[edge:high] = jnp.zeros((step - depth, right.shape[1]), right.dtype)
 
     square_sum = jnp.zeros(sq_ref.shape, jnp.float32) if fresh else refs[1][...]
     for c, (a, row, _) in enumerate(spots):
         wide = blocks[a][row].astype(jnp.float32)
         square_sum += jnp.sum((wide * wide).reshape(-1, 8, wide.shape[1]), axis=0)
-        right[c * step : c * step + depth] = (wide * gains[c][0]).astype(right.dtype)
+        column = gains[c][0].T[:, :1]
+        right[c * step : c * step + depth] = (wide * column).astype(right.dtype)
     sq_ref[...] = square_sum
     made = jnp.dot(left[...], right[...], preferred_element_type=jnp.float32)
     acc_ref[...] = made if fresh else made + refs[0][...]
@@ -119,21 +130,22 @@
 def project_in(spots, table, blocks, gate, up, gain, sums):
     count = len(spots)
     depth, rows = blocks[0].shape[1:]
-    units, step = gate.shape[1:]
+    units = gate.shape[1]
+    step = PADDED
     keep = pl.BlockSpec((2 * units, ROW_TILE), lambda i, t: (0, i))
     keep_sq = pl.BlockSpec((8, ROW_TILE), lambda i, t: (0, i))
 
     def picked(shape):
         return [
-            pl.BlockSpec((1,) + shape, lambda i, t, k=k, j=j: (t[k, j], 0, 0))
-            for _, _, (k, j) in spots
+            pl.BlockSpec((1,) + shape, lambda i, t, m=m, k=k, j=j: (t[m, k, j], 0, 0))
+            for _, _, (m, k, j) in spots
         ]
 
     in_specs = [
         pl.BlockSpec((b.shape[0], depth, ROW_TILE), lambda i, t: (0, 0, i)) for b in blocks
     ]
-    in_specs += picked((units, step)) + picked((units, step)) + picked((depth, 1))
-    args = [table] + list(blocks) + [gate] * count + [up] * count + [gain] * count
+    in_specs += [pl.BlockSpec(memory_space=pltpu.HBM)] * 2 + picked((8, depth))
+    args = [table] + list(blocks) + [gate, up] + [gain] * count
     if sums is not None:
         in_specs += [keep, keep_sq]
         args += list(sums)
@@ -151,9 +163,11 @@
             scratch_shapes=[
                 pltpu.VMEM((2 * units, count * step), jnp.bfloat16),
                 pltpu.VMEM((count * step, ROW_TILE), jnp.bfloat16),
+                pltpu.VMEM((count, 2, units, depth), jnp.bfloat16),
+                pltpu.SemaphoreType.DMA((count, 2)),
             ],
         ),
-        compiler_params=pltpu.CompilerParams(vmem_limit_bytes=32 * 2**20),
+        compiler_params=pltpu.CompilerParams(vmem_limit_bytes=46 * 2**20),
         cost_estimate=pl.CostEstimate(
             flops=4 * count * depth * rows * units,
             bytes_accessed=2 * count * depth * (rows + 2 * units),
@@ -284,11 +298,11 @@
     limit = capacity[expert].astype(jnp.float32)
     row_weight = jnp.where(position < limit, gate_of, 0.0)
 
-    gain = norm_gain.reshape(-1, column_width, 1)
+    gain = norm_gain.reshape(-1, 1, column_width)
+    gain = jnp.broadcast_to(gain, (gain.shape[0], 8, column_width))
 
     def turned(table):
-        blocks = jnp.swapaxes(table.reshape(-1, column_width, hidden), 1, 2)
-        return jnp.pad(blocks, ((0, 0), (0, 0), (0, PADDED - column_width)))
+        return jnp.swapaxes(table.reshape(-1, column_width, hidden), 1, 2)
 
     gate, up = turned(w_gate[0]), turned(w_up[0])
     down = w_down[0].T.reshape(-1, column_width, hidden)
@@ -326,34 +340,34 @@
     def swap(block):
         return shift(block, PAIRS, 1)
 
-    def add_in(spots, table, blocks, sums):
-        return project_in(spots, table, blocks, gate, up, gain, sums)
-
-    here = ((0, 0, (0, 0)),) + tuple((1, j - 1, (0, j)) for j in range(1, SIDE))
-    ones = tuple((0, k - 1, (k, 0)) for k in range(1, SIDE))
-
-    def rest(*steps):
-        return tuple(
-            (a, j - 1, (k, j)) for a, k in enumerate(steps) for j in range(1, SIDE)
-        )
-
-    own = [columns[None], inner]
-    mate = [swap(columns)[None], swap(inner)]
-    sums = add_in(here, own_in, own, None)
-    sums = add_in(here, mate_in, mate, sums)
+    def add_in(spots, blocks, sums):
+        return project_in(spots, tables_in, blocks, gate, up, gain, sums)
+
+    tables_in = jnp.stack([own_in, mate_in])
+
+    def here(m, a):
+        lone = ((a, 0, (m, 0, 0)),)
+        return lone + tuple((a + 1, j - 1, (m, 0, j)) for j in range(1, SIDE))
+
+    def ones(m, a):
+        return tuple((a, k - 1, (m, k, 0)) for k in range(1, SIDE))
+
+    def rest(m, a, k):
+        return tuple((a, j - 1, (m, k, j)) for j in range(1, SIDE))
+
+    blocks = [columns[None], inner, swap(columns)[None], swap(inner)]
     heads_of = jnp.stack([first[k] for k in range(1, SIDE)])
-    heads_of, sums = lax.optimization_barrier((heads_of, sums))
-    mate = swap(heads_of)
-    sums = add_in(ones, own_in, [heads_of], sums)
-    sums = add_in(ones, mate_in, [mate], sums)
+    blocks += [heads_of, swap(heads_of)]
+    spots = here(0, 0) + here(1, 2) + ones(0, 4) + ones(1, 5)
+    sums = add_in(spots, blocks, None)
     second[2], sums = lax.optimization_barrier((second[2], sums))
-    mate = swap(second[2])
-    sums = add_in(rest(2), own_in, [second[2]], sums)
-    sums = add_in(rest(2), mate_in, [mate], sums)
+    blocks = [second[2], swap(second[2])]
+    sums = add_in(rest(0, 0, 2) + rest(1, 1, 2), blocks, sums)
     second[1], second[3], sums = lax.optimization_barrier((second[1], second[3], sums))
-    mate = [swap(second[1]), swap(second[3])]
-    sums = add_in(rest(1, 3), own_in, [second[1], second[3]], sums)
-    sums = add_in(rest(1, 3), mate_in, mate, sums)
+    blocks = [second[1], second[3]]
+    blocks += [swap(second[1]), swap(second[3])]
+    spots = rest(0, 0, 1) + rest(0, 1, 3) + rest(1, 2, 1) + rest(1, 3, 3)
+    sums = add_in(spots, blocks, sums)
     total, squares = sums
     mean_square = jnp.sum(squares, axis=0, keepdims=True) / model_width
     pre = total * lax.rsqrt(mean_square + epsilon)

time: 242 us -> 231 us (0.955)
  local copies, waits for them, and re-layouts: 44.4 us -> 25.5 us
  starting transfers between devices: 48.9 us -> 57.8 us
    ppermute x28, starting transfers between devices: 28.4 us -> 39.4 us  [shift(): return lax.ppermute(block, 'expert', pairs)]
    pad x2 -> x0, local copies, waits for them, and re-layouts: 8.33 us -> none  [turned(): return jnp.pad(blocks, ((0, 0), (0, 0), (0, PADDED - column_width)))]
    unnamed x31 -> x17, local copies, waits for them, and re-layouts: 9.83 us -> 1.81 us
    ppermute x28, waiting for transfers between devices: 52.8 us -> 49.9 us  [shift(): return lax.ppermute(block, 'expert', pairs)]
    optimization_barrier x1 -> x0, local copies, waits for them, and re-layouts: 2.45 us -> none  [shards(): held = lax.optimization_barrier(held)]
    pallas_call x8 -> x3, Pallas kernels: 22.8 us -> 22.6 us  [project_in(): pl.pallas_call(functools.partial(in_body, spots, sums is None), out_shape...]
  transfers between devices with their start and end apart: 31 -> 31, of which waited for: 13 -> 15; matrix products, arithmetic and copies ran while one was open for 14% -> 9% of each run, Pallas kernels for 12% -> 11%
where the time goes in v2:
time: 231 us; the launch traced here: 228 us
  waiting for transfers between devices  65.8 us (28%)
  starting transfers between devices  57.8 us (25%)
  Pallas kernels  36.2 us (16%)
  blocking collectives  33.5 us (15%)
  local copies, waits for them, and re-layouts  25.5 us (11%)
  matrix products  4.41 us (2%)
  other arithmetic  3.33 us (1%)
    ppermute x28, waiting for transfers between devices, shift(): return lax.ppermute(block, 'expert', pairs)  49.9 us
    ppermute x28, starting transfers between devices, shift(): return lax.ppermute(block, 'expert', pairs)  39.4 us
    pallas_call x3, Pallas kernels, project_in(): pl.pallas_call(functools.partial(in_body, spots, sums is None), out_shape...  22.6 us
    all_to_all x1, blocking collectives, shards(): combined = add_blocks(lax.all_to_all(parts, 'tensor', 0, 0, tiled=True))  17.8 us
    all_to_all x2, blocking collectives, exchange(): lax.all_to_all(blocks, 'expert', 0, 0, axis_index_groups=groups, tiled=True)  15.7 us
    pallas_call x8, Pallas kernels, project_out(): pl.pallas_call(out_body if mate is None else out_add_body, out_shape=out_...  13.6 us
    another operation x2, local copies, waits for them, and re-layouts, turned(): return jnp.swapaxes(table.reshape(-1, column_width, hidden), 1, 2)  12.6 us
    all_to_all x1, starting transfers between devices, shards(): lax.all_to_all(partial_out.astype(jnp.bfloat16), 'tensor', 0, 0, tiled=True)  8.47 us
  transfers between devices with their start and end apart: 31, of which 15 were waited for; matrix products, arithmetic and copies ran while one was open for 9% of the time, Pallas kernels for 11%

profile of v2, /device:TPU:2, one launch (start us, length us, event | category | flops | bytes accessed | tf_op | source)
XLA Modules:
  0.0 227.6 jit_solution(13689139342603557514)
XLA Ops:
  4.5 10.6 %all_to_all.30 = bf16[4,24,1024]{2,1,0:T(8,128)(2,1)S(1)} all-to-all(bf16[4,24,1024]{2,1,0:T(8,128)(2,1)S(1)} %broadcast_in_dim.72), channel_id=1, replica_groups={{0,2,4,6},{8,10,12,14},{16,18,20,22},{24,26,28,30},{1,9,17,25},{3,11,19..., dimensions={0} | all-to-all | bytes 393216 | tf_op jit(solution)/shard_map/all_to_all | solution.py:37
  16.1 4.8 %all-to-all-start.1 = ((bf16[4,4,24,1024]{3,2,1,0:T(8,128)(2,1)}), bf16[4,4,24,1024]{3,2,1,0:T(8,128)(2,1)S(1)}, u32[]{:S(2)}, u32[]{:S(2)}) async-start(bf16[4,4,24,1024]{3,2,1,0:T(8,128)(2,1)} %broadcast_in_dim.73), calls=%async_computation.1 | async-start | bytes 1572864 | tf_op jit(solution)/shard_map/all_to_all | solution.py:37
  21.9 7.0 %all-to-all-done.1 = bf16[4,4,24,1024]{3,2,1,0:T(8,128)(2,1)S(1)} async-done(((bf16[4,4,24,1024]{3,2,1,0:T(8,128)(2,1)}), bf16[4,4,24,1024]{3,2,1,0:T(8,128)(2,1)S(1)}, u32[]{:S(2)}, u32[]{:S(2)}) %all-to-all-start.1) | async-done | bytes 786464 | tf_op jit(solution)/shard_map/all_to_all | solution.py:37
  29.1 5.1 %all_to_all.31 = bf16[2,4,4,24,1024]{4,3,2,1,0:T(8,128)(2,1)S(1)} all-to-all(bf16[2,4,4,24,1024]{4,3,2,1,0:T(8,128)(2,1)S(1)} %broadcast_in_dim.74), channel_id=1, replica_groups={{0,1},{2,3},{4,5},{6,7},{8,9},{10,11},{12,13},{14,15},{16,17},{18,19},{..., dimensions={0} | all-to-all | bytes 3145728 | tf_op jit(solution)/shard_map/all_to_all | solution.py:37
  36.2 8.5 %all-to-all-start.3 = ((bf16[8,96,224]{2,1,0:T(8,128)(2,1)}), bf16[8,96,224]{2,1,0:T(8,128)(2,1)S(1)}, u32[]{:S(2)}, u32[]{:S(2)}) async-start(bf16[8,96,224]{2,1,0:T(8,128)(2,1)} %bitcast.6), calls=%async_computation.3 | async-start | bytes 786432 | tf_op jit(solution)/shard_map/all_to_all | solution.py:317
  44.8 6.3 %copy.36 = bf16[32,224,256]{1,2,0:T(8,128)(2,1)} copy(bf16[32,224,256]{2,1,0:T(8,128)(2,1)} %bitcast.86) | data formatting | bytes 7340032 | tf_op jit(solution)/shard_map/reshape;squeeze | solution.py:305
  51.1 6.3 %copy.35 = bf16[32,224,256]{1,2,0:T(8,128)(2,1)} copy(bf16[32,224,256]{2,1,0:T(8,128)(2,1)} %bitcast.87) | data formatting | bytes 7340032 | tf_op jit(solution)/shard_map/reshape;squeeze | solution.py:305
  60.5 5.1 %all-to-all-start.4 = ((bf16[8,96,224]{2,1,0:T(8,128)(2,1)}), bf16[8,96,224]{2,1,0:T(8,128)(2,1)S(1)}, u32[]{:S(2)}, u32[]{:S(2)}) async-start(bf16[8,96,224]{2,1,0:T(8,128)(2,1)} %broadcast_in_dim.75), calls=%async_computation.4 | async-start | bytes 786432 | tf_op jit(solution)/shard_map/all_to_all | solution.py:322
  66.9 5.8 %copy.37 = bf16[7168,256]{1,0:T(8,128)(2,1)} copy(bf16[7168,256]{0,1:T(8,128)(2,1)} %bitcast.85) | data formatting | bytes 7340032 | tf_op jit(solution)/shard_map/transpose | solution.py:308
  73.2 6.8 %all-to-all-done.4 = bf16[8,96,224]{2,1,0:T(8,128)(2,1)S(1)} async-done(((bf16[8,96,224]{2,1,0:T(8,128)(2,1)}), bf16[8,96,224]{2,1,0:T(8,128)(2,1)S(1)}, u32[]{:S(2)}, u32[]{:S(2)}) %all-to-all-start.4) | async-done | bytes 344096 | tf_op jit(solution)/shard_map/all_to_all | solution.py:322
  80.3 3.5 %collective-permute-start.9 = (bf16[224,768]{1,0:T(8,128)(2,1)S(1)}, bf16[224,768]{1,0:T(8,128)(2,1)S(1)}, u32[]{:S(2)}, u32[]{:S(2)}) collective-permute-start(bf16[224,768]{1,0:T(8,128)(2,1)S(1)} %bitcast.70), channel_id=1, source_target_pairs={{0,16},{8,24},{16,0},{24,8},{2,18},{10,26},{18,2},{26,10},{4,20},{... | collective-permute-start | bytes 1032200 | tf_op jit(solution)/shard_map/ppermute | solution.py:55
  87.0 4.0 %collective-permute-done.8 = bf16[224,768]{1,0:T(8,128)(2,1)S(1)} collective-permute-done((bf16[224,768]{1,0:T(8,128)(2,1)S(1)}, bf16[224,768]{1,0:T(8,128)(2,1)S(1)}, u32[]{:S(2)}, u32[]{:S(2)}) %collective-permute-start.8) | collective-permute-done | bytes 344096 | tf_op jit(solution)/shard_map/ppermute | solution.py:55
  92.8 7.3 %collective-permute-done.10 = bf16[224,768]{1,0:T(8,128)(2,1)S(1)} collective-permute-done((bf16[224,768]{1,0:T(8,128)(2,1)S(1)}, bf16[224,768]{1,0:T(8,128)(2,1)S(1)}, u32[]{:S(2)}, u32[]{:S(2)}) %collective-permute-start.10) | collective-permute-done | bytes 344096 | tf_op jit(solution)/shard_map/ppermute | solution.py:55
  101.0 4.6 %collective-permute-start.5 = (bf16[3,224,768]{2,1,0:T(8,128)(2,1)S(1)}, bf16[3,224,768]{2,1,0:T(8,128)(2,1)S(1)}, u32[]{:S(2)}, u32[]{:S(2)}) collective-permute-start(bf16[3,224,768]{2,1,0:T(8,128)(2,1)S(1)} %pad_maximum_fusion.refs_1_), channel_id=1, source_target_pairs={{0,16},{8,24},{16,0},{24,8},{2,18},{10,26},{18,2},{26,10},{4,20},{... | collective-permute-start | bytes 3096584 | tf_op jit(solution)/shard_map/ppermute | solution.py:55
  107.3 8.8 %shard_map.127 = (f32[512,768]{1,0:T(8,128)S(1)}, f32[8,768]{1,0:T(8,128)S(1)}) custom-call(s32[2,4,4]{2,1,0:T(4,128)S(1)} %pad_add_fusion.table, bf16[1,224,768]{2,1,0:T(8,128)(2,1)S(1)} %bitcast.76, bf16[3,224,768]{2,1,0:T(8,128)(2,1)S(1)} %pad_maximum_fusion.refs_1_, bf16[1,224,768]{2,1,0:T(8,128)(2,1)S(1)} %bitcast.77, ...), custom_call_target="tpu_custom_call" | custom-call | flops 2466250752 | bytes 8028160 | tf_op jit(solution)/shard_map/pallas_call | solution.py:152
  118.2 4.4 %collective-permute-start.3 = (bf16[3,224,768]{2,1,0:T(8,128)(2,1)S(1)}, bf16[3,224,768]{2,1,0:T(8,128)(2,1)S(1)}, u32[]{:S(2)}, u32[]{:S(2)}) collective-permute-start(bf16[3,224,768]{2,1,0:T(8,128)(2,1)S(1)} %pad_maximum_fusion.refs_1_), channel_id=1, source_target_pairs={{0,8},{8,16},{16,24},{24,0},{2,10},{10,18},{18,26},{26,2},{4,12},{... | collective-permute-start | bytes 3096584 | tf_op jit(solution)/shard_map/ppermute | solution.py:55
  124.7 5.4 %shard_map.128 = (f32[512,768]{1,0:T(8,128)S(1)}, f32[8,768]{1,0:T(8,128)S(1)}) custom-call(s32[2,4,4]{2,1,0:T(4,128)S(1)} %pad_add_fusion.table, bf16[3,224,768]{2,1,0:T(8,128)(2,1)S(1)} %collective-permute-done.5.refs_0_, bf16[3,224,768]{2,1,0:T(8,128)(2,1)S(1)} %collective-permute-done.12.refs_1_, bf16[32,256,224]{2,1,0:T(8,128)(2,1)} %bitcast.83, ...), custom_call_target="tpu_custom_call" | custom-call | flops 1056964608 | bytes 3440640 | tf_op jit(solution)/shard_map/pallas_call | solution.py:152
  130.1 7.2 %collective-permute-done.3.refs_0_ = bf16[3,224,768]{2,1,0:T(8,128)(2,1)S(1)} collective-permute-done((bf16[3,224,768]{2,1,0:T(8,128)(2,1)S(1)}, bf16[3,224,768]{2,1,0:T(8,128)(2,1)S(1)}, u32[]{:S(2)}, u32[]{:S(2)}) %collective-permute-start.3) | collective-permute-done | bytes 1032224 | tf_op jit(solution)/shard_map/ppermute | solution.py:55
  141.4 8.5 %shard_map.129 = (f32[512,768]{1,0:T(8,128)S(1)}, f32[8,768]{1,0:T(8,128)S(1)}) custom-call(s32[2,4,4]{2,1,0:T(4,128)S(1)} %pad_add_fusion.table, bf16[3,224,768]{2,1,0:T(8,128)(2,1)S(1)} %collective-permute-done.3.refs_0_, bf16[3,224,768]{2,1,0:T(8,128)(2,1)S(1)} %collective-permute-done.4.refs_1_, ...), custom_call_target="tpu_custom_call" | custom-call | flops 2113929216 | bytes 6881280 | tf_op jit(solution)/shard_map/pallas_call | solution.py:152
  180.4 3.2 %collective-permute-start.21 = (bf16[224,768]{1,0:T(8,128)(2,1)S(1)}, bf16[224,768]{1,0:T(8,128)(2,1)S(1)}, u32[]{:S(2)}, u32[]{:S(2)}) collective-permute-start(bf16[224,768]{1,0:T(8,128)(2,1)S(1)} %get-tuple-element.82), channel_id=1, source_target_pairs={{0,24},{8,0},{16,8},{24,16},{2,26},{10,2},{18,10},{26,18},{4,28},{... | collective-permute-start | bytes 1032200 | tf_op jit(solution)/shard_map/ppermute | solution.py:55
  183.7 10.7 %collective-permute-done.24 = bf16[3,224,768]{2,1,0:T(8,128)(2,1)S(1)} collective-permute-done((bf16[3,224,768]{2,1,0:T(8,128)(2,1)S(1)}, bf16[3,224,768]{2,1,0:T(8,128)(2,1)S(1)}, u32[]{:S(2)}, u32[]{:S(2)}) %collective-permute-start.24) | collective-permute-done | bytes 1032224 | tf_op jit(solution)/shard_map/ppermute | solution.py:55
  194.8 3.9 %collective-permute-start.26 = (bf16[224,768]{1,0:T(8,128)(2,1)S(1)}, bf16[224,768]{1,0:T(8,128)(2,1)S(1)}, u32[]{:S(2)}, u32[]{:S(2)}) collective-permute-start(bf16[224,768]{1,0:T(8,128)(2,1)S(1)} %get-tuple-element.91), channel_id=1, source_target_pairs={{0,4},{2,6},{4,0},{6,2},{8,12},{10,14},{12,8},{14,10},{16,20},{18,... | collective-permute-start | bytes 1032200 | tf_op jit(solution)/shard_map/ppermute | solution.py:55
  198.7 9.7 %collective-permute-done.21 = bf16[224,768]{1,0:T(8,128)(2,1)S(1)} collective-permute-done((bf16[224,768]{1,0:T(8,128)(2,1)S(1)}, bf16[224,768]{1,0:T(8,128)(2,1)S(1)}, u32[]{:S(2)}, u32[]{:S(2)}) %collective-permute-start.21) | collective-permute-done | bytes 344096 | tf_op jit(solution)/shard_map/ppermute | solution.py:55
  209.1 17.8 %all_to_all.32 = bf16[8,96,224]{2,1,0:T(8,128)(2,1)S(1)} all-to-all(bf16[8,96,224]{2,1,0:T(8,128)(2,1)S(1)} %bitcast.90), channel_id=1, replica_groups=mesh['tensor'=8,'expert'=32] {'tensor'}, dimensions={0} | all-to-all | bytes 688128 | tf_op jit(solution)/shard_map/all_to_all | solution.py:402
  (126 shorter events, 61.1 us)
Async XLA Ops:
  16.1 12.9 %all-to-all-start.1 = ((bf16[4,4,24,1024]{3,2,1,0:T(8,128)(2,1)}), bf16[4,4,24,1024]{3,2,1,0:T(8,128)(2,1)S(1)}, u32[]{:S(2)}, u32[]{:S(2)}) async-start(bf16[4,4,24,1024]{3,2,1,0:T(8,128)(2,1)} %broadcast_in_dim.73), calls=%async_computation.1 | async-start | bytes 1572864 | tf_op jit(solution)/shard_map/all_to_all | solution.py:37
  36.2 23.5 %all-to-all-start.3 = ((bf16[8,96,224]{2,1,0:T(8,128)(2,1)}), bf16[8,96,224]{2,1,0:T(8,128)(2,1)S(1)}, u32[]{:S(2)}, u32[]{:S(2)}) async-start(bf16[8,96,224]{2,1,0:T(8,128)(2,1)} %bitcast.6), calls=%async_computation.3 | async-start | bytes 786432 | tf_op jit(solution)/shard_map/all_to_all | solution.py:317
  60.5 19.5 %all-to-all-start.4 = ((bf16[8,96,224]{2,1,0:T(8,128)(2,1)}), bf16[8,96,224]{2,1,0:T(8,128)(2,1)S(1)}, u32[]{:S(2)}, u32[]{:S(2)}) async-start(bf16[8,96,224]{2,1,0:T(8,128)(2,1)} %broadcast_in_dim.75), calls=%async_computation.4 | async-start | bytes 786432 | tf_op jit(solution)/shard_map/all_to_all | solution.py:322
  80.2 10.8 %collective-permute-start.8 = (bf16[224,768]{1,0:T(8,128)(2,1)S(1)}, bf16[224,768]{1,0:T(8,128)(2,1)S(1)}, u32[]{:S(2)}, u32[]{:S(2)}) collective-permute-start(bf16[224,768]{1,0:T(8,128)(2,1)S(1)} %bitcast.69), channel_id=1, source_target_pairs={{0,8},{8,16},{16,24},{24,0},{2,10},{10,18},{18,26},{26,2},{4,12},{... | collective-permute-start | bytes 1032200 | tf_op jit(solution)/shard_map/ppermute | solution.py:55
  80.3 12.5 %collective-permute-start.9 = (bf16[224,768]{1,0:T(8,128)(2,1)S(1)}, bf16[224,768]{1,0:T(8,128)(2,1)S(1)}, u32[]{:S(2)}, u32[]{:S(2)}) collective-permute-start(bf16[224,768]{1,0:T(8,128)(2,1)S(1)} %bitcast.70), channel_id=1, source_target_pairs={{0,16},{8,24},{16,0},{24,8},{2,18},{10,26},{18,2},{26,10},{4,20},{... | collective-permute-start | bytes 1032200 | tf_op jit(solution)/shard_map/ppermute | solution.py:55
  83.8 16.3 %collective-permute-start.10 = (bf16[224,768]{1,0:T(8,128)(2,1)S(1)}, bf16[224,768]{1,0:T(8,128)(2,1)S(1)}, u32[]{:S(2)}, u32[]{:S(2)}) collective-permute-start(bf16[224,768]{1,0:T(8,128)(2,1)S(1)} %bitcast.71), channel_id=1, source_target_pairs={{0,24},{8,0},{16,8},{24,16},{2,26},{10,2},{18,10},{26,18},{4,28},{... | collective-permute-start | bytes 1032200 | tf_op jit(solution)/shard_map/ppermute | solution.py:55
  84.4 15.9 %collective-permute-start = (bf16[224,768]{1,0:T(8,128)(2,1)S(1)}, bf16[224,768]{1,0:T(8,128)(2,1)S(1)}, u32[]{:S(2)}, u32[]{:S(2)}) collective-permute-start(bf16[224,768]{1,0:T(8,128)(2,1)S(1)} %bitcast.72), channel_id=1, source_target_pairs={{0,2},{2,4},{4,6},{6,0},{8,10},{10,12},{12,14},{14,8},{16,18},{18,... | collective-permute-start | bytes 1032200 | tf_op jit(solution)/shard_map/ppermute | solution.py:55
  84.9 15.4 %collective-permute-start.1 = (bf16[224,768]{1,0:T(8,128)(2,1)S(1)}, bf16[224,768]{1,0:T(8,128)(2,1)S(1)}, u32[]{:S(2)}, u32[]{:S(2)}) collective-permute-start(bf16[224,768]{1,0:T(8,128)(2,1)S(1)} %bitcast.73), channel_id=1, source_target_pairs={{0,4},{2,6},{4,0},{6,2},{8,12},{10,14},{12,8},{14,10},{16,20},{18,... | collective-permute-start | bytes 1032200 | tf_op jit(solution)/shard_map/ppermute | solution.py:55
  91.0 9.4 %collective-permute-start.2 = (bf16[224,768]{1,0:T(8,128)(2,1)S(1)}, bf16[224,768]{1,0:T(8,128)(2,1)S(1)}, u32[]{:S(2)}, u32[]{:S(2)}) collective-permute-start(bf16[224,768]{1,0:T(8,128)(2,1)S(1)} %bitcast.74), channel_id=1, source_target_pairs={{0,6},{2,0},{4,2},{6,4},{8,14},{10,8},{12,10},{14,12},{16,22},{18,... | collective-permute-start | bytes 1032200 | tf_op jit(solution)/shard_map/ppermute | solution.py:55
  100.2 7.1 %collective-permute-start.11 = (bf16[3,224,768]{2,1,0:T(8,128)(2,1)S(1)}, bf16[3,224,768]{2,1,0:T(8,128)(2,1)S(1)}, u32[]{:S(2)}, u32[]{:S(2)}) collective-permute-start(bf16[3,224,768]{2,1,0:T(8,128)(2,1)S(1)} %pad_maximum_fusion.1.refs_4_), channel_id=1, source_target_pairs={{0,1},{1,0},{2,3},{3,2},{4,5},{5,4},{6,7},{7,6},{8,9},{9,8},{10,11... | collective-permute-start | bytes 3096584 | tf_op jit(solution)/shard_map/ppermute | solution.py:55
  101.0 17.2 %collective-permute-start.5 = (bf16[3,224,768]{2,1,0:T(8,128)(2,1)S(1)}, bf16[3,224,768]{2,1,0:T(8,128)(2,1)S(1)}, u32[]{:S(2)}, u32[]{:S(2)}) collective-permute-start(bf16[3,224,768]{2,1,0:T(8,128)(2,1)S(1)} %pad_maximum_fusion.refs_1_), channel_id=1, source_target_pairs={{0,16},{8,24},{16,0},{24,8},{2,18},{10,26},{18,2},{26,10},{4,20},{... | collective-permute-start | bytes 3096584 | tf_op jit(solution)/shard_map/ppermute | solution.py:55
  118.2 19.1 %collective-permute-start.3 = (bf16[3,224,768]{2,1,0:T(8,128)(2,1)S(1)}, bf16[3,224,768]{2,1,0:T(8,128)(2,1)S(1)}, u32[]{:S(2)}, u32[]{:S(2)}) collective-permute-start(bf16[3,224,768]{2,1,0:T(8,128)(2,1)S(1)} %pad_maximum_fusion.refs_1_), channel_id=1, source_target_pairs={{0,8},{8,16},{16,24},{24,0},{2,10},{10,18},{18,26},{26,2},{4,12},{... | collective-permute-start | bytes 3096584 | tf_op jit(solution)/shard_map/ppermute | solution.py:55
  122.7 14.7 %collective-permute-start.4 = (bf16[3,224,768]{2,1,0:T(8,128)(2,1)S(1)}, bf16[3,224,768]{2,1,0:T(8,128)(2,1)S(1)}, u32[]{:S(2)}, u32[]{:S(2)}) collective-permute-start(bf16[3,224,768]{2,1,0:T(8,128)(2,1)S(1)} %pad_maximum_fusion.refs_1_), channel_id=1, source_target_pairs={{0,24},{8,0},{16,8},{24,16},{2,26},{10,2},{18,10},{26,18},{4,28},{... | collective-permute-start | bytes 3096584 | tf_op jit(solution)/shard_map/ppermute | solution.py:55
  160.3 9.6 %collective-permute-start.17 = (bf16[4,224,768]{2,1,0:T(8,128)(2,1)S(1)}, bf16[4,224,768]{2,1,0:T(8,128)(2,1)S(1)}, u32[]{:S(2)}, u32[]{:S(2)}) collective-permute-start(bf16[4,224,768]{2,1,0:T(8,128)(2,1)S(1)} %shard_map.134), channel_id=1, source_target_pairs={{0,1},{1,0},{2,3},{3,2},{4,5},{5,4},{6,7},{7,6},{8,9},{9,8},{10,11... | collective-permute-start | bytes 4128776 | tf_op jit(solution)/shard_map/ppermute | solution.py:55
  163.9 10.5 %collective-permute-start.18 = (bf16[4,224,768]{2,1,0:T(8,128)(2,1)S(1)}, bf16[4,224,768]{2,1,0:T(8,128)(2,1)S(1)}, u32[]{:S(2)}, u32[]{:S(2)}) collective-permute-start(bf16[4,224,768]{2,1,0:T(8,128)(2,1)S(1)} %shard_map.136), channel_id=1, source_target_pairs={{0,1},{1,0},{2,3},{3,2},{4,5},{5,4},{6,7},{7,6},{8,9},{9,8},{10,11... | collective-permute-start | bytes 4128776 | tf_op jit(solution)/shard_map/ppermute | solution.py:55
  164.6 15.8 %collective-permute-start.22 = (bf16[3,224,768]{2,1,0:T(8,128)(2,1)S(1)}, bf16[3,224,768]{2,1,0:T(8,128)(2,1)S(1)}, u32[]{:S(2)}, u32[]{:S(2)}) collective-permute-start(bf16[3,224,768]{2,1,0:T(8,128)(2,1)S(1)} %get-tuple-element.84), channel_id=1, source_target_pairs={{0,8},{8,16},{16,24},{24,0},{2,10},{10,18},{18,26},{26,2},{4,12},{... | collective-permute-start | bytes 3096584 | tf_op jit(solution)/shard_map/ppermute | solution.py:55
  167.2 16.4 %collective-permute-start.23 = (bf16[3,224,768]{2,1,0:T(8,128)(2,1)S(1)}, bf16[3,224,768]{2,1,0:T(8,128)(2,1)S(1)}, u32[]{:S(2)}, u32[]{:S(2)}) collective-permute-start(bf16[3,224,768]{2,1,0:T(8,128)(2,1)S(1)} %get-tuple-element.85), channel_id=1, source_target_pairs={{0,16},{8,24},{16,0},{24,8},{2,18},{10,26},{18,2},{26,10},{4,20},{... | collective-permute-start | bytes 3096584 | tf_op jit(solution)/shard_map/ppermute | solution.py:55
  171.7 22.7 %collective-permute-start.24 = (bf16[3,224,768]{2,1,0:T(8,128)(2,1)S(1)}, bf16[3,224,768]{2,1,0:T(8,128)(2,1)S(1)}, u32[]{:S(2)}, u32[]{:S(2)}) collective-permute-start(bf16[3,224,768]{2,1,0:T(8,128)(2,1)S(1)} %get-tuple-element.86), channel_id=1, source_target_pairs={{0,24},{8,0},{16,8},{24,16},{2,26},{10,2},{18,10},{26,18},{4,28},{... | collective-permute-start | bytes 3096584 | tf_op jit(solution)/shard_map/ppermute | solution.py:55
  174.4 24.4 %collective-permute-start.19 = (bf16[224,768]{1,0:T(8,128)(2,1)S(1)}, bf16[224,768]{1,0:T(8,128)(2,1)S(1)}, u32[]{:S(2)}, u32[]{:S(2)}) collective-permute-start(bf16[224,768]{1,0:T(8,128)(2,1)S(1)} %get-tuple-element.80), channel_id=1, source_target_pairs={{0,8},{8,16},{16,24},{24,0},{2,10},{10,18},{18,26},{26,2},{4,12},{... | collective-permute-start | bytes 1032200 | tf_op jit(solution)/shard_map/ppermute | solution.py:55
  174.4 24.4 %collective-permute-start.20 = (bf16[224,768]{1,0:T(8,128)(2,1)S(1)}, bf16[224,768]{1,0:T(8,128)(2,1)S(1)}, u32[]{:S(2)}, u32[]{:S(2)}) collective-permute-start(bf16[224,768]{1,0:T(8,128)(2,1)S(1)} %get-tuple-element.81), channel_id=1, source_target_pairs={{0,16},{8,24},{16,0},{24,8},{2,18},{10,26},{18,2},{26,10},{4,20},{... | collective-permute-start | bytes 1032200 | tf_op jit(solution)/shard_map/ppermute | solution.py:55
  180.4 28.0 %collective-permute-start.21 = (bf16[224,768]{1,0:T(8,128)(2,1)S(1)}, bf16[224,768]{1,0:T(8,128)(2,1)S(1)}, u32[]{:S(2)}, u32[]{:S(2)}) collective-permute-start(bf16[224,768]{1,0:T(8,128)(2,1)S(1)} %get-tuple-element.82), channel_id=1, source_target_pairs={{0,24},{8,0},{16,8},{24,16},{2,26},{10,2},{18,10},{26,18},{4,28},{... | collective-permute-start | bytes 1032200 | tf_op jit(solution)/shard_map/ppermute | solution.py:55
  194.7 14.0 %collective-permute-start.25 = (bf16[224,768]{1,0:T(8,128)(2,1)S(1)}, bf16[224,768]{1,0:T(8,128)(2,1)S(1)}, u32[]{:S(2)}, u32[]{:S(2)}) collective-permute-start(bf16[224,768]{1,0:T(8,128)(2,1)S(1)} %get-tuple-element.89), channel_id=1, source_target_pairs={{0,2},{2,4},{4,6},{6,0},{8,10},{10,12},{12,14},{14,8},{16,18},{18,... | collective-permute-start | bytes 1032200 | tf_op jit(solution)/shard_map/ppermute | solution.py:55
  194.8 13.9 %collective-permute-start.26 = (bf16[224,768]{1,0:T(8,128)(2,1)S(1)}, bf16[224,768]{1,0:T(8,128)(2,1)S(1)}, u32[]{:S(2)}, u32[]{:S(2)}) collective-permute-start(bf16[224,768]{1,0:T(8,128)(2,1)S(1)} %get-tuple-element.91), channel_id=1, source_target_pairs={{0,4},{2,6},{4,0},{6,2},{8,12},{10,14},{12,8},{14,10},{16,20},{18,... | collective-permute-start | bytes 1032200 | tf_op jit(solution)/shard_map/ppermute | solution.py:55
  198.7 9.9 %collective-permute-start.27 = (bf16[224,768]{1,0:T(8,128)(2,1)S(1)}, bf16[224,768]{1,0:T(8,128)(2,1)S(1)}, u32[]{:S(2)}, u32[]{:S(2)}) collective-permute-start(bf16[224,768]{1,0:T(8,128)(2,1)S(1)} %get-tuple-element.90), channel_id=1, source_target_pairs={{0,6},{2,0},{4,2},{6,4},{8,14},{10,8},{12,10},{14,12},{16,22},{18,... | collective-permute-start | bytes 1032200 | tf_op jit(solution)/shard_map/ppermute | solution.py:55
  (15 other events, 87.1 us)
